TPU v7x, 128 devices: a whole 4x4x4 slice. The times are simulated.
128 devices in a mesh: lon: 16 (over x, z), lat: 8 (over y, core).
Axes of the slice: x: 4, y: 4, z: 4, core: 2. Of those that a mesh axis runs over, the one named last changes fastest.
Arguments:
- state: float32 [8, 64, 32, 2048], P(None, None, 'lat', 'lon'), may hold values from -6 to 6
- winds: float32 [2, 64, 32, 2048], P(None, None, 'lat', 'lon'), may hold values from -0.3 to 0.3
- diffusivity: float32 [32, 2048], P('lat', 'lon'), may hold values from 0.05 to 0.2
- sounding_cell: int32 [2, 16384], P(None, ('lon', 'lat')), may hold values from 0 to 511
- sounding_owner: int32 [2, 16384, 1], P(None, ('lon', 'lat')), may hold values from 0 to 127; in each aligned block of 128 rows (0 to 127, 128 to 255, ..., all dimensions but the last counted through in order) at most 3 rows name the same one
- step_counts: int32 [2], replicated, may hold values from 1 to 4
- channel_list: int32 [512], replicated, may hold values from 0 to 615
- absorb_table: float32 [512, 616], replicated, may hold values from -0.25 to 0.25
- emit_table: float32 [512, 616], replicated, may hold values from -0.25 to 0.25
- obs_weight: float32 [616], replicated, may hold values from 0.5 to 4
- observed: float32 [2, 128, 128, 3, 512], P(None, ('lon', 'lat')), may hold values from -6 to 6
Outputs:
- gradient: float32 [8, 64, 32, 2048], P(None, None, 'lat', 'lon')
Inputs may be any that keep to these rules, and one draw needn't show every extreme that they name: `sounding_owner`: in one slot, at most 3 soundings of one tile's list name the same owner. `sounding_cell`: columns are numbered row by row within the tile. `channel_list`: entries may repeat.
All inputs are finite; a program needn't handle non-finite values.
Results may differ from a plain program's by a relative error of at most 0.00022.
Values sent between devices are 32-bit elements; how exact they have to be, the bound alone decides.
No kernel may reach another device: no remote copies, remote signals or barrier semaphores. Data moves between devices by JAX's collectives and lax.ppermute only.
A program may use at most 128 MiB of HBM per device.

v0:
```python
from functools import partial

import jax
import jax.numpy as jnp
from jax import lax
from jax.experimental import pallas as pl
from jax.experimental.pallas import tpu as pltpu
from jax.sharding import PartitionSpec as P

F32 = jnp.float32
BF16 = jnp.bfloat16
I32 = jnp.int32
VARS = 8
SPAN = 32
STRIP_SPAN = 16
LEV = 64
MAXSTEP = 4
SND = 128


def struct(*shape, dtype=F32):
    return jax.ShapeDtypeStruct(shape, dtype)


def tiled(grid, *shape):
    zeros = (0,) * (len(shape) - 2)
    return pl.BlockSpec((*shape[:-2], shape[-2] // grid, shape[-1]), lambda t: (*zeros, t, 0))


def whole(shape):
    return pl.BlockSpec(shape, lambda *_: (0,) * len(shape))


VMEM_SPEC = pl.BlockSpec(memory_space=pltpu.VMEM)
SMEM_SPEC = pl.BlockSpec(memory_space=pltpu.SMEM)


def params(mebibytes):
    return pltpu.CompilerParams(vmem_limit_bytes=mebibytes * 1024 * 1024)


def in_hbm(*arrays):
    return [pltpu.with_memory_space_constraint(x, pltpu.HBM) for x in arrays]


def lanes():
    return lax.broadcasted_iota(I32, (STRIP_SPAN, 128), 1)


def roll(x, shift):
    shift = shift % 128
    return x if shift == 0 else pltpu.roll(x, shift, 1)


def level_tiles(count, body, span=8):
    def step(t, carry):
        body(t, pl.ds(pl.multiple_of(t * span, span), span))
        return carry

    lax.fori_loop(0, count, step, 0)


def lon_even():
    return lax.axis_index("lon") % 2 == 0


def lat_even():
    return lax.axis_index("lat") % 2 == 0


def own_strip(load, count):
    lane = lanes()
    strip = jnp.zeros((STRIP_SPAN, 128), F32)
    for g in range(count):
        x = load(g)
        base = 32 * g
        strip = jnp.where((lane >= base + 8) & (lane < base + 16), roll(x, base + 8), strip)
        strip = jnp.where((lane >= base + 16) & (lane < base + 24), roll(x, base + 24), strip)
    return strip


def pack_strips(strips, even):
    lane = lanes() % 32
    east = jnp.zeros((STRIP_SPAN, 128), F32)
    west = jnp.zeros((STRIP_SPAN, 128), F32)
    for r in range(4):
        here = (lane >= 8 * r) & (lane < 8 * r + 8)
        east = jnp.where(here, roll(strips[r], 8 * r - 16), east)
        west = jnp.where(here, roll(strips[r], 8 * r - 8), west)
    return jnp.where(even, east, west), jnp.where(even, west, east)


def pack_kernel(state, winds, diff, main, strip, first, second, *, grid):
    even = lon_even()
    flip = jnp.where(lat_even(), 3, 0)

    def body(t, level):
        strips = [[] for _ in range(3)]
        for p in range(4):
            r = jnp.abs(flip - p)
            source = pl.ds(t * 4 * STRIP_SPAN + r, STRIP_SPAN, stride=4)
            row = [state[v, source, :] for v in range(VARS)] + [winds[v, source, :] for v in range(2)]
            row.append(jnp.broadcast_to(diff[pl.ds(r, 1), :], (STRIP_SPAN, 128)))
            for v in range(11):
                main[p, v, level, :] = row[v]
            for b in range(3):
                s = own_strip(lambda g: row[4 * b + g], 4 if b < 2 else 3)
                strip[p, b, level, :] = s
                strips[b].append(s)
        for b in range(3):
            first[b, level, :], second[b, level, :] = pack_strips(strips[b], even)

    level_tiles(LEV // STRIP_SPAN // grid, body, STRIP_SPAN)


def pack(state, winds, diff, grid=2):
    shapes = [(4, 11, LEV, 128), (4, 3, LEV, 128), (3, LEV, 128), (3, LEV, 128)]
    return pl.pallas_call(
        partial(pack_kernel, grid=grid),
        grid=(grid,),
        in_specs=[tiled(grid, 8, 256, 128), tiled(grid, 2, 256, 128), whole((4, 128))],
        out_specs=[tiled(grid, *s) for s in shapes],
        out_shape=[struct(*s) for s in shapes],
        compiler_params=params(16),
        name="pack",
    )(*in_hbm(state, winds), diff)


def complete_kernel(strip, first, second, *outs):
    even = lon_even()
    blocks = strip.shape[1]
    split = blocks // len(outs)

    def body(t, level):
        lane = lax.broadcasted_iota(I32, (SPAN, 128), 1) % 32
        for b in range(blocks):
            one, two = first[b, level, :], second[b, level, :]
            east = jnp.where(even, one, two)
            west = jnp.where(even, two, one)
            for r in range(4):
                full = jnp.where(lane < 8, roll(west, -8 * r), strip[r, b, level, :])
                outs[b // split][r, b % split, level, :] = jnp.where(lane >= 24, roll(east, 24 - 8 * r), full)

    level_tiles(LEV // SPAN, body, SPAN)


def complete(strip, first, second, parts):
    split = strip.shape[1] // parts
    return pl.pallas_call(
        complete_kernel,
        in_specs=[VMEM_SPEC] * 3,
        out_specs=[VMEM_SPEC] * parts,
        out_shape=[struct(4, split, LEV, 128)] * parts,
        compiler_params=params(4),
        name="complete",
    )(strip, first, second)


def open_to_next_chip():
    lat = lax.axis_index("lat")
    return jnp.where((lat > 0) & (lat < lax.axis_size("lat") - 1), 1.0, 0.0).astype(F32)


def each_row(first, last, body):
    def step(i, carry):
        body(i)
        return carry

    lax.fori_loop(first, last, step, 0)


def coefficient_kernel(own, r0, r1, sown, s0, s1, out, raw):
    flipped = lat_even()
    open_side = open_to_next_chip()
    lane = lax.broadcasted_iota(I32, (LEV, 128), 1)

    def fill(i, main, strip):
        packed = strip[2]
        spread = []
        for g in range(3):
            one = jnp.where(lane < 32, roll(packed, -32 * g), 0.0)
            one = one + roll(one, 32)
            spread.append(one + roll(one, 64))
        plain = [main[VARS], main[VARS + 1], main[VARS + 2]]
        for n, (w0, w1, dd) in enumerate((plain, spread)):
            half = w0 * 0.5
            half_west, dd_west = roll(half, 1), roll(dd, 1)
            if n == 0:
                half_west = jnp.where(lane == 0, roll(spread[0], 121) * 0.5, half_west)
                dd_west = jnp.where(lane == 0, roll(spread[2], 121), dd_west)
            a, b = half + dd, half - dd
            a_west, b_west = half_west + dd_west, half_west - dd_west
            half = w1 * 0.5
            for m, value in enumerate((a, b_west, half + dd, half - dd)):
                raw[i, 4 * n + m] = value
            out[i, 5 * n] = 1.0 - a + b_west
            out[i, 5 * n + 1] = -b
            out[i, 5 * n + 2] = a_west

    each_row(0, 4, lambda j: fill(3 - j, r0.at[j], s0.at[j]))
    each_row(0, 4, lambda j: fill(4 + j, own.at[j], sown.at[j]))
    each_row(0, 4, lambda j: fill(8 + j, r1.at[3 - j], s1.at[3 - j]))

    def interface(i):
        for n in range(2):
            c, d = raw[i, 4 * n + 2], raw[i, 4 * n + 3]
            c_next, d_next = raw[i + 1, 4 * n + 2], raw[i + 1, 4 * n + 3]
            raw[i, 4 * n + 2] = jnp.where(flipped, -d_next, c)
            raw[i, 4 * n + 3] = jnp.where(flipped, -c_next, d)

    each_row(0, 11, interface)

    def combine(i):
        scale = jnp.where(i >= 8, open_side, 1.0)
        for n in range(2):
            u, w = raw[i, 4 * n + 2], raw[i, 4 * n + 3]
            u_before, w_before = raw[i - 1, 4 * n + 2], raw[i - 1, 4 * n + 3]
            out[i, 5 * n] = (out[i, 5 * n] - u + w_before) * scale
            out[i, 5 * n + 1] = out[i, 5 * n + 1] * scale
            out[i, 5 * n + 2] = out[i, 5 * n + 2] * scale
            out[i, 5 * n + 3] = -w * scale
            out[i, 5 * n + 4] = u_before * scale

    each_row(1, 11, combine)


def coefficients(tile, strips):
    return pl.pallas_call(
        coefficient_kernel,
        in_specs=[VMEM_SPEC] * 6,
        out_specs=[VMEM_SPEC] * 2,
        out_shape=[struct(12, 10, LEV, 128), struct(12, 8, LEV, 128)],
        compiler_params=params(4),
        name="coefficients",
    )(*tile, *strips)


def adjoint_kernel(forward, raw, out):
    open_side = open_to_next_chip()

    def combine(i):
        scale = jnp.where(i >= 8, open_side, 1.0)
        for n in range(2):
            out[i, 5 * n] = forward[i, 5 * n]
            out[i, 5 * n + 1] = raw[i, 4 * n] * scale
            out[i, 5 * n + 2] = -raw[i, 4 * n + 1] * scale
            out[i, 5 * n + 3] = raw[i, 4 * n + 2] * scale
            out[i, 5 * n + 4] = -raw[i - 1, 4 * n + 3] * scale

    each_row(1, 11, combine)


def adjoint_coefficients(forward, raw):
    return pl.pallas_call(
        adjoint_kernel,
        in_specs=[VMEM_SPEC] * 2,
        out_specs=VMEM_SPEC,
        out_shape=struct(12, 10, LEV, 128),
        compiler_params=params(4),
        name="adjoint_coefficients",
    )(forward, raw)


def advect_kernel(*refs, steps, apart, result, addend):
    refs = list(refs)
    steps = refs.pop(0)[0] if steps is None else steps
    own, r0, r1 = refs[:3]
    refs = refs[3:]
    strips = ()
    if apart:
        strips, refs = refs[:3], refs[3:]
    coef = refs.pop(0)
    if addend:
        add_main, add_strip = refs[:2]
        refs = refs[2:]
    out, *work, shift = refs
    source = lax.broadcasted_iota(I32, (256, 256), 0) % 128
    target = lax.broadcasted_iota(I32, (256, 256), 1)
    chosen = jnp.where(target < 128, target + 1, target + 127) % 128
    shift[...] = (source == chosen).astype(F32).astype(BF16)
    flip = jnp.where(lat_even(), 3, 0)
    width = r0.shape[0]

    def place(target, sources, offset, count):
        tile, intra, inter = sources

        def halo(j, carry):
            target[3 - j, offset : offset + count] = intra[j, 0:count]
            target[8 + j, offset : offset + count] = inter[width - 1 - j, 0:count]
            return carry

        def inside(j, carry):
            target[4 + j, offset : offset + count] = tile[j, 0:count]
            return carry

        lax.fori_loop(0, width, halo, 0)
        lax.fori_loop(0, 4, inside, 0)

    def start(target):
        if apart:
            place(target, (own, r0, r1), 0, VARS)
            place(target, strips, VARS, 2)
        else:
            place(target, (own, r0, r1), 0, VARS + 2)

    def when(condition, run):
        if isinstance(condition, bool):
            if condition:
                run()
        else:
            pl.when(condition)(run)

    for n in range(2):
        when(steps % 2 != n, partial(start, work[n]))
    lane = lax.broadcasted_iota(I32, (LEV, 128), 1)

    def row(now, i, last, store):
        def stencil(n, v, f, east, west):
            value = coef[i, n] * f
            value = value + coef[i, n + 1] * east
            value = value + coef[i, n + 2] * west
            value = value + coef[i, n + 3] * now[i + 1, v]
            return value + coef[i, n + 4] * now[i - 1, v]

        wanted = VARS + (0 if last and result != "both" else 2)
        halves = split(now[i, 0:wanted].reshape(wanted * LEV, 128))
        moved = dot(jnp.concatenate(halves, axis=1), shift[...], (1, 0))
        moved = moved.reshape(wanted, LEV, 256)
        for b in range(2):
            f = now[i, VARS + b]
            ends = jnp.where(lane % 32 == 25, roll(f, 18), f)
            for v in (VARS + b, *range(4 * b, 4 * b + 4)):
                if v >= wanted:
                    continue
                f = now[i, v]
                east, west = moved[v, :, :128], moved[v, :, 128:]
                if v < VARS:
                    rim = roll(ends, 103 - 32 * (v % 4))
                    east = jnp.where(lane == 127, rim, east)
                    west = jnp.where(lane == 0, rim, west)
                store(v, stencil(5 if v >= VARS else 0, v, f, east, west))

    def step(reach):
        def one(i, carry):
            def store(v, value):
                work[1 - reach % 2][i, v] = value

            row(work[reach % 2], i, False, store)
            return carry

        lax.fori_loop(4 - reach, 8 + reach, one, 0)

    for reach in (3, 2, 1):
        when(steps > reach, partial(step, reach))

    def final(r, carry):
        def store(v, value):
            if addend:
                value = value + (add_main[r, v] if v < VARS else add_strip[r, v - VARS])
            if result == "native":
                out[v, pl.ds(jnp.abs(flip - r), LEV, stride=4), :] = value
            else:
                out[r, v] = value

        row(work[0], 4 + r, True, store)
        return carry

    lax.fori_loop(0, 4, final, 0)


def advect(steps, tile, strips, coef, result, addend=None):
    args = [*tile]
    if strips is not None:
        args += strips
    args.append(coef)
    if addend is not None:
        args += addend
    if result == "native":
        shape = (8, 256, 128)
    else:
        shape = (4, 10 if result == "both" else 8, LEV, 128)
    static = isinstance(steps, int)
    return pl.pallas_call(
        partial(
            advect_kernel,
            steps=steps if static else None,
            apart=strips is not None,
            result=result,
            addend=addend is not None,
        ),
        in_specs=([] if static else [SMEM_SPEC]) + [VMEM_SPEC] * len(args),
        out_specs=VMEM_SPEC,
        out_shape=struct(*shape),
        scratch_shapes=[pltpu.VMEM((12, 10, LEV, 128), F32)] * 2 + [pltpu.VMEM((256, 256), BF16)],
        compiler_params=params(14),
        name="advect_" + result,
    )(*([] if static else [steps]), *args)


def split(x):
    high = x.astype(BF16)
    return high, (x - high.astype(F32)).astype(BF16)


def dot(x, y, dims):
    return lax.dot_general(x, y, ((dims[:1], dims[1:]), ((), ())), preferred_element_type=F32)


def dot3(x, y, dims):
    return dot(x[0], y[0], dims) + (dot(x[0], y[1], dims) + dot(x[1], y[0], dims))


def relayout_kernel(observed, sent):
    homes = observed.shape[3]
    for k in range(2):
        for q in range(3):
            for c in range(4):
                sent[pl.ds(12 * k + 4 * q + c, homes, stride=24), :] = observed[k, 0, q, :, pl.ds(128 * c, 128)]


def relayout(observed):
    turned = jnp.transpose(observed, (0, 1, 3, 2, 4))
    homes = turned.shape[3]
    sent = pl.pallas_call(
        relayout_kernel,
        grid=(1,),
        in_specs=[whole(turned.shape)],
        out_specs=whole((homes * 24, 128)),
        out_shape=struct(homes * 24, 128),
        compiler_params=params(16),
        name="relayout",
    )(*in_hbm(turned))
    return sent.reshape(homes, 24, 128)


PADDED = 640


def column_of(row):
    square = (SND, SND)
    here = lax.broadcasted_iota(I32, square, 0) == lax.broadcasted_iota(I32, square, 1)
    return jnp.sum(jnp.where(here, jnp.broadcast_to(row, square), 0), axis=1, keepdims=True)


def load_table(table, high, low):
    count = table.shape[0]
    full = count // 16 * 16
    high[pl.ds(0, full), :], low[pl.ds(0, full), :] = split(table[pl.ds(0, full), :])
    rest = jnp.zeros((PADDED - full, table.shape[1]), F32)
    if count > full:
        zeros = jnp.zeros((PADDED - count, table.shape[1]), F32)
        rest = jnp.concatenate([table[pl.ds(full, count - full), :], zeros], axis=0)
    high[pl.ds(full, PADDED - full), :], low[pl.ds(full, PADDED - full), :] = split(rest)


def observe_kernel(cells, owners, channels, weight, field, *refs, slot):
    if slot == 0:
        hbm, refs = refs[:3], refs[3:]
        (out, strip, first, second, *tables), refs = refs[:8], refs[8:]
        (absorb_table, emit_table, fetched), sems = refs[:3], refs[3]
        targets = (absorb_table, emit_table, fetched)
    else:
        tables, hbm, before, refs = refs[:4], refs[4:5], refs[5:8], refs[8:]
        (out, strip, first, second), (fetched, sems) = refs[:4], refs[4:]
        targets = (fetched,)
    copies = [
        pltpu.make_async_copy(source, target, sems.at[n])
        for n, (source, target) in enumerate(zip(hbm, targets, strict=True))
    ]
    for copy in copies:
        copy.start()

    flip = jnp.where(lat_even(), 3, 0)
    square = (SND, SND)
    row_id = lax.broadcasted_iota(I32, square, 0)
    lane_id = lax.broadcasted_iota(I32, square, 1)
    entry = lax.broadcasted_iota(I32, (PADDED, channels.shape[1]), 0)
    listed = (entry == channels[...]).astype(F32).astype(BF16)
    times = dot(jnp.ones((8, channels.shape[1]), BF16), listed, (1, 1))[0:1]
    cell = column_of(cells[slot : slot + 1, :])
    owner_row = owners[slot : slot + 1, :]
    owner = column_of(owner_row)
    earlier = (owner == owner_row) & (lane_id < row_id)
    rank = jnp.sum(jnp.where(earlier, 1, 0), axis=1, keepdims=True)
    picks = [(cell == lane_id + 128 * jnp.abs(flip - r)).astype(F32).astype(BF16) for r in range(4)]
    pieces = [jnp.zeros((SND, VARS * LEV), F32)] * 2
    for r in range(4):
        x = split(field[r, 0:VARS].reshape(VARS * LEV, 128))
        pieces = [piece + dot(picks[r], part, (1, 1)) for piece, part in zip(pieces, x, strict=True)]
    column = [piece.astype(BF16) for piece in pieces]
    if slot == 0:
        for n, table in enumerate((absorb_table, emit_table)):
            copies[n].wait()
            load_table(table, tables[2 * n], tables[2 * n + 1])
    absorb = (tables[0][...], tables[1][...])
    emission = (tables[2][...], tables[3][...])
    optical = dot3(column, absorb, (1, 1))
    bright = dot3(column, emission, (1, 1))
    decay = jnp.exp(-jnp.abs(optical))
    inverse = 1.0 / (1.0 + decay)
    rest = decay * inverse
    positive = optical >= 0
    passing = jnp.where(positive, rest, inverse)
    opaque = jnp.where(positive, inverse, rest)
    choices = [((owner == lane_id) & (rank == q)).astype(F32).astype(BF16) for q in range(3)]
    copies[-1].wait()
    parts = []
    for c in range(4):
        part = [jnp.zeros(square, F32)] * 2
        for q in range(3):
            seen = split(fetched[pl.ds(12 * slot + 4 * q + c, SND, stride=24), :])
            part = [p + dot(choices[q], x, (1, 0)) for p, x in zip(part, seen, strict=True)]
        parts.append(part)
    wanted = [jnp.concatenate([part[n] for part in parts], axis=1).astype(BF16) for n in range(2)]
    totals = dot(wanted[0], listed, (1, 1)) + dot(wanted[1], listed, (1, 1))
    evolved = passing * bright
    departure = weight[...] * (times * evolved - totals)
    to_bright = departure * passing
    to_optical = -(departure * evolved * opaque)
    column = dot3(split(to_optical), absorb, (1, 0)) + dot3(split(to_bright), emission, (1, 0))
    ch, cl = split(column)
    for r in range(4):
        placed = dot(ch, picks[r], (0, 0)) + dot(cl, picks[r], (0, 0))
        out[r] = placed.reshape(VARS, LEV, 128)

    even = lon_even()
    if slot == 1:
        strip[:, 2:4] = before[0][...]
        first[2:4] = before[1][...]
        second[2:4] = before[2][...]

    def strips_of(t, level):
        for b in range(2):
            strips = []
            for r in range(4):
                s = own_strip(lambda g: out[r, 4 * b + g, level, :], 4)
                strip[r, b, level, :] = s
                strips.append(s)
            first[b, level, :], second[b, level, :] = pack_strips(strips, even)

    level_tiles(LEV // STRIP_SPAN, strips_of, STRIP_SPAN)


def observe(slot, small, field, tables, fetched, before):
    count = 2 if slot == 0 else 4
    shapes = [struct(4, 8, LEV, 128), struct(4, count, LEV, 128)] + [struct(count, LEV, 128)] * 2
    moved = [fetched]
    if slot == 0:
        moved = [*tables, fetched]
        tables = []
        shapes += [struct(PADDED, VARS * LEV, dtype=BF16)] * 4
    hbm_spec = pl.BlockSpec(memory_space=pltpu.HBM)
    return pl.pallas_call(
        partial(observe_kernel, slot=slot),
        in_specs=[VMEM_SPEC] * (len(small) + 1 + len(tables)) + [hbm_spec] * len(moved) + [VMEM_SPEC] * len(before),
        out_specs=[VMEM_SPEC] * len(shapes),
        out_shape=shapes,
        scratch_shapes=[pltpu.VMEM(x.shape, F32) for x in moved] + [pltpu.SemaphoreType.DMA((len(moved),))],
        compiler_params=params(10),
        name="observe",
    )(*small, field, *tables, *in_hbm(*moved), *before)


def swap(x, axis, parity, wrap):
    devices = lax.axis_size(axis)
    pairs = []
    for i in range(parity, devices, 2):
        if i + 1 < devices or wrap:
            j = (i + 1) % devices
            pairs += [(i, j), (j, i)]
    return lax.ppermute(x, axis, pairs)


def lat_swap(x, width=4):
    beyond = swap(x[4 - width :], "lat", 1, False)
    return swap(x[:width], "lat", 0, False), beyond


def lon_swap(first, second):
    beyond = swap(second, "lon", 1, True)
    return swap(first, "lon", 0, True), beyond


def per_device(
    state, winds, diffusivity, sounding_cell, sounding_owner, step_counts, channel_list, absorb_table, emit_table,
    obs_weight, observed,
):
    def by_steps(slot, run):
        branches = [partial(run, width) for width in range(1, MAXSTEP + 1)]
        return lax.switch(step_counts[slot] - 1, branches)

    main, strip, first, second = pack(state.reshape(8, 256, 128), winds.reshape(2, 256, 128), diffusivity)
    received = lon_swap(first, second)
    halo = lat_swap(main)
    sent, received = lax.optimization_barrier((relayout(observed), received))
    (strip,) = complete(strip, *received, 1)
    fetched = lax.all_to_all(sent, ("lon", "lat"), split_axis=0, concat_axis=0, tiled=True)
    tile, strips = (main, *halo), (strip, *lat_swap(strip))
    onward, raw = coefficients(tile, strips)
    both0 = advect(step_counts[:1], tile, strips, onward, "both")
    halo = lat_swap(both0)
    raw, both0 = lax.optimization_barrier((raw, both0))
    backward_coef = adjoint_coefficients(onward, raw)

    extra = PADDED - obs_weight.shape[0]
    padded_weight = jnp.pad(obs_weight, (0, extra))[None, :]
    small = [sounding_cell, sounding_owner[:, :, 0], channel_list[None, :], padded_weight]
    fetched = fetched.reshape(-1, 128)
    g0, *edges, th0, tl0, th1, tl1 = observe(0, small, both0, [absorb_table.T, emit_table.T], fetched, [])
    both0, backward_coef, g0 = lax.optimization_barrier((both0, backward_coef, g0))
    field1 = advect(step_counts[1:], (both0, *halo), None, onward, "main")
    g1, strip, first, second = observe(1, small, field1, [th0, tl0, th1, tl1], fetched, edges)

    def backward(width):
        received = lon_swap(first, second)
        halo = lat_swap(g1, width)
        strips1, strips0 = complete(strip, *received, 2)
        halo_strips = lat_swap(strips1, width)
        return advect(width, (g1, *halo), (strips1, *halo_strips), backward_coef, "both", (g0, strips0))

    both = by_steps(1, backward)

    def last(width):
        return advect(width, (both, *lat_swap(both, width)), None, backward_coef, "native")

    result = by_steps(0, last)
    return result.reshape(state.shape)


def solution(mesh):
    return jax.shard_map(
        per_device,
        mesh=mesh,
        in_specs=(
            P(None, None, "lat", "lon"),
            P(None, None, "lat", "lon"),
            P("lat", "lon"),
            P(None, ("lon", "lat")),
            P(None, ("lon", "lat"), None),
            P(),
            P(),
            P(),
            P(),
            P(),
            P(None, ("lon", "lat"), None, None, None),
        ),
        out_specs=P(None, None, "lat", "lon"),
        check_vma=False,
    )
```

profile of v0, /device:TPU:1, one launch (start us, length us, event | category | flops | bytes accessed | tf_op | source)
XLA Modules:
  0.0 125.3 jit_solution(3902679122110727246)
XLA Ops:
  0.0 0.7 copy-done.7
  0.7 2.6 %pack.1 = (f32[4,11,64,128]{3,2,1,0:T(8,128)S(1)}, f32[4,3,64,128]{3,2,1,0:T(8,128)S(1)}, f32[3,64,128]{2,1,0:T(8,128)S(1)}, f32[3,64,128]{2,1,0:T(8,128)S(1)}) custom-call(f32[8,256,128]{2,1,0:T(8,128)} %bitcast.22, f32[2,256,128]{2,1,0:T(8,128)} %bitcast.27, f32[4,128]{1,0:T(4,128)S(1)} %copy-done.7), custom_call_target="tpu_custom_call" | custom-call | tf_op jit(solution)/shard_map/pack/pallas_call | solution.py:118
  3.3 1.5 %collective-permute-start.32 = (f32[4,11,64,128]{3,2,1,0:T(8,128)S(1)}, f32[4,11,64,128]{3,2,1,0:T(8,128)}, u32[]{:S(2)}, u32[]{:S(2)}) collective-permute-start(f32[4,11,64,128]{3,2,1,0:T(8,128)S(1)} %get-tuple-element.146.own.refs_1_), channel_id=1, source_target_pairs={{0,1},{1,0},{2,3},{3,2},{4,5},{5,4},{6,7},{7,6},{8,9},{9,8},{10,11... | collective-permute-start | bytes 4325384 | tf_op jit(solution)/shard_map/ppermute | solution.py:571
  4.8 3.2 %collective-permute-start.33 = (f32[4,11,64,128]{3,2,1,0:T(8,128)S(1)}, f32[4,11,64,128]{3,2,1,0:T(8,128)}, u32[]{:S(2)}, u32[]{:S(2)}) collective-permute-start(f32[4,11,64,128]{3,2,1,0:T(8,128)S(1)} %get-tuple-element.146.own.refs_1_), channel_id=1, source_target_pairs={{1,2},{2,1},{3,4},{4,3},{5,6},{6,5},{9,10},{10,9},{11,12},{12,11},... | collective-permute-start | bytes 4325384 | tf_op jit(solution)/shard_map/ppermute | solution.py:571
  8.0 1.7 %collective-permute-start.34 = (f32[3,64,128]{2,1,0:T(8,128)S(1)}, f32[3,64,128]{2,1,0:T(8,128)S(1)}, u32[]{:S(2)}, u32[]{:S(2)}) collective-permute-start(f32[3,64,128]{2,1,0:T(8,128)S(1)} %get-tuple-element.148), channel_id=1, source_target_pairs={{0,8},{8,0},{16,24},{24,16},{32,40},{40,32},{48,56},{56,48},{64,72... | collective-permute-start | bytes 294920 | tf_op jit(solution)/shard_map/ppermute | solution.py:571
  9.7 4.4 %collective-permute-start.35 = (f32[3,64,128]{2,1,0:T(8,128)S(1)}, f32[3,64,128]{2,1,0:T(8,128)S(1)}, u32[]{:S(2)}, u32[]{:S(2)}) collective-permute-start(f32[3,64,128]{2,1,0:T(8,128)S(1)} %get-tuple-element.149), channel_id=1, source_target_pairs={{8,16},{16,8},{24,32},{32,24},{40,48},{48,40},{56,64},{64,56},{72,... | collective-permute-start | bytes 294920 | tf_op jit(solution)/shard_map/ppermute | solution.py:571
  14.1 2.9 %relayout.1 = f32[3072,128]{1,0:T(8,128)} custom-call(f32[2,1,3,128,512]{4,3,2,1,0:T(8,128)} %bitcast.19), custom_call_target="tpu_custom_call" | custom-call | tf_op jit(solution)/shard_map/relayout/pallas_call | solution.py:424
  17.1 0.0 collective-permute-done.34.first
  17.1 0.0 collective-permute-done.35.second
  17.1 0.3 complete.9.sown.refs_4_
  17.4 0.0 copy-start.12
  17.4 0.1 collective-permute-start.36
  17.5 4.3 %collective-permute-start.37 = (f32[4,3,64,128]{3,2,1,0:T(8,128)S(1)}, f32[4,3,64,128]{3,2,1,0:T(8,128)S(1)}, u32[]{:S(2)}, u32[]{:S(2)}) collective-permute-start(f32[4,3,64,128]{3,2,1,0:T(8,128)S(1)} %complete.9.sown.refs_4_), channel_id=1, source_target_pairs={{1,2},{2,1},{3,4},{4,3},{5,6},{6,5},{9,10},{10,9},{11,12},{12,11},... | collective-permute-start | bytes 1179656 | tf_op jit(solution)/shard_map/ppermute | solution.py:571
  21.7 8.0 %all-to-all-start = ((f32[128,24,128]{2,1,0:T(8,128)}), f32[128,24,128]{2,1,0:T(8,128)}, u32[]{:S(2)}, u32[]{:S(2)}) async-start(f32[128,24,128]{2,1,0:T(8,128)} %bitcast.11), calls=%async_computation | async-start | bytes 3145728 | tf_op jit(solution)/shard_map/all_to_all | solution.py:597
  29.7 0.0 copy-done.12
  29.7 0.6 fusion.9
  30.3 0.0 collective-permute-done.36.s0.refs_5_
  30.3 0.0 collective-permute-done.37.s1.refs_6_
  30.3 0.0 collective-permute-done.32.r0.refs_2_
  30.3 0.0 collective-permute-done.33.r1.refs_3_
  30.4 5.9 %coefficients.1 = (f32[12,10,64,128]{3,2,1,0:T(8,128)S(1)}, f32[12,8,64,128]{3,2,1,0:T(8,128)S(1)}) custom-call(f32[4,11,64,128]{3,2,1,0:T(8,128)S(1)} %get-tuple-element.146.own.refs_1_, f32[4,11,64,128]{3,2,1,0:T(8,128)} %collective-permute-done.32.r0.refs_2_, f32[4,11,64,128]{3,2,1,0:T(8,128)} %collective-permute-done.33.r1.refs_3_, ...), custom_call_target="tpu_custom_call" | custom-call | tf_op jit(solution)/shard_map/coefficients/pallas_call | solution.py:228
  36.3 0.0 copy-done.2
  36.3 0.0 copy-start
  36.3 0.0 copy-start.3
  36.3 1.3 %copy-done.3 = f32[4,3,64,128]{3,2,1,0:T(8,128)S(1)} copy-done((f32[4,3,64,128]{3,2,1,0:T(8,128)S(1)}, f32[4,3,64,128]{3,2,1,0:T(8,128)}, u32[]{:S(2)}) %copy-start.3) | copy-done | bytes 393240
  37.6 4.1 %advect_both.9.field.refs_1_ = f32[4,10,64,128]{3,2,1,0:T(8,128)S(1)} custom-call(s32[1]{0:T(128)} %get-tuple-element.192.refs_0_, f32[4,11,64,128]{3,2,1,0:T(8,128)S(1)} %get-tuple-element.146.own.refs_1_, f32[4,11,64,128]{3,2,1,0:T(8,128)} %collective-permute-done.32.r0.refs_2_, f32[4,11,64,128]{3,2,1,0:T(8,128)} %collective-permute-done.33.r1.refs_3_, ...), custom_call_target="tpu_custom_call" | custom-call | tf_op jit(solution)/shard_map/advect_both/pallas_call | solution.py:383
  41.7 1.2 collective-permute-start.38
  42.9 2.6 %collective-permute-start.39 = (f32[4,10,64,128]{3,2,1,0:T(8,128)S(1)}, f32[4,10,64,128]{3,2,1,0:T(8,128)}, u32[]{:S(2)}, u32[]{:S(2)}) collective-permute-start(f32[4,10,64,128]{3,2,1,0:T(8,128)S(1)} %advect_both.9.field.refs_1_), channel_id=1, source_target_pairs={{1,2},{2,1},{3,4},{4,3},{5,6},{6,5},{9,10},{10,9},{11,12},{12,11},... | collective-permute-start | bytes 3932168 | tf_op jit(solution)/shard_map/ppermute | solution.py:571
  46.8 0.0 copy-start.4
  46.8 0.0 copy-start.5
  46.8 0.0 copy-start.6
  46.8 2.2 %adjoint_coefficients.1 = f32[12,10,64,128]{3,2,1,0:T(8,128)} custom-call(f32[12,10,64,128]{3,2,1,0:T(8,128)S(1)} %get-tuple-element.153.refs_7_.forward.refs_4_, f32[12,8,64,128]{3,2,1,0:T(8,128)S(1)} %get-tuple-element.155.raw), custom_call_target="tpu_custom_call" | custom-call | tf_op jit(solution)/shard_map/adjoint_coefficients/pallas_call | solution.py:254
  49.0 5.1 %all-to-all-done = f32[128,24,128]{2,1,0:T(8,128)} async-done(((f32[128,24,128]{2,1,0:T(8,128)}), f32[128,24,128]{2,1,0:T(8,128)}, u32[]{:S(2)}, u32[]{:S(2)}) %all-to-all-start) | async-done | bytes 1572896 | tf_op jit(solution)/shard_map/all_to_all | solution.py:597
  54.1 0.0 copy-done.4
  54.1 7.5 %observe.2 = (f32[4,8,64,128]{3,2,1,0:T(8,128)S(1)}, f32[4,2,64,128]{3,2,1,0:T(8,128)S(1)}, f32[2,64,128]{2,1,0:T(8,128)S(1)}, f32[2,64,128]{2,1,0:T(8,128)S(1)}...) custom-call(s32[2,128]{1,0:T(2,128)S(1)} %copy-done.5, ...), custom_call_target="tpu_custom_call" | custom-call | tf_op jit(solution)/shard_map/observe/pallas_call | solution.py:553
  61.7 0.0 collective-permute-done.38.refs_2_
  61.7 1.4 %collective-permute-done.39.refs_3_ = f32[4,10,64,128]{3,2,1,0:T(8,128)} collective-permute-done((f32[4,10,64,128]{3,2,1,0:T(8,128)S(1)}, f32[4,10,64,128]{3,2,1,0:T(8,128)}, u32[]{:S(2)}, u32[]{:S(2)}) %collective-permute-start.39) | collective-permute-done | bytes 1310752 | tf_op jit(solution)/shard_map/ppermute | solution.py:571
  63.1 11.0 %advect_main.1.field = f32[4,8,64,128]{3,2,1,0:T(8,128)S(1)} custom-call(s32[1]{0:T(128)} %get-tuple-element.191.refs_0_, f32[4,10,64,128]{3,2,1,0:T(8,128)S(1)} %advect_both.9.field.refs_1_, f32[4,10,64,128]{3,2,1,0:T(8,128)S(1)} %collective-permute-done.38.refs_2_, f32[4,10,64,128]{3,2,1,0:T(8,128)} %collective-permute-done.39.refs_3_, ...), custom_call_target="tpu_custom_call" | custom-call | tf_op jit(solution)/shard_map/advect_main/pallas_call | solution.py:383
  74.1 6.9 %observe.3 = (f32[4,8,64,128]{3,2,1,0:T(8,128)S(1)}, f32[4,4,64,128]{3,2,1,0:T(8,128)S(1)}, f32[4,64,128]{2,1,0:T(8,128)S(1)}, f32[4,64,128]{2,1,0:T(8,128)S(1)}) custom-call(s32[2,128]{1,0:T(2,128)S(1)} %copy-done.5, s32[2,128]{1,0:T(2,128)S(1)} %bitcast.18, s32[1,512]{1,0:T(1,128)S(1)} %bitcast.16, f32[1,640]{1,0:T(1,128)S(1)} %broadcast_in_dim.7.weight, ...), custom_call_target="tpu_custom_call" | custom-call | tf_op jit(solution)/shard_map/observe/pallas_call | solution.py:553
  81.0 0.0 copy-done.8
  81.0 30.9 %conditional.2 = (f32[4,10,64,128]{3,2,1,0:T(8,128)S(1)}) conditional(s32[]{:T(128)} %bitcast.5, (f32[4,8,64,128]{3,2,1,0:T(8,128)S(1)}, f32[4,64,128]{2,1,0:T(8,128)S(1)}, f32[4,64,128]{2,1,0:T(8,128)S(1)}, f32[4,4,64,128]{3,2,1,0:T(8,128)S(1)}, f32[12,10,64,128]{3,2,1,0:T(8,128)S(1)}, ...), branch_computations={%region_0.1_spmd, %region_1.2_spmd, %region_2.3_spmd, %region_3.4_... | conditional | bytes 12845304 | solution.py:590
  81.0 0.1 collective-permute-start
  81.1 3.9 %collective-permute-start.1 = (f32[4,8,64,128]{3,2,1,0:T(8,128)S(1)}, f32[4,8,64,128]{3,2,1,0:T(8,128)S(1)}, u32[]{:S(2)}, u32[]{:S(2)}) collective-permute-start(f32[4,8,64,128]{3,2,1,0:T(8,128)S(1)} %get-tuple-element.104.refs_0_), channel_id=1, source_target_pairs={{1,2},{2,1},{3,4},{4,3},{5,6},{6,5},{9,10},{10,9},{11,12},{12,11},... | collective-permute-start | bytes 3145736 | tf_op jit(solution)/shard_map/cond/branch_3_fun/ppermute | solution.py:571
  85.1 1.1 collective-permute-start.2
  86.2 3.5 %collective-permute-start.3 = (f32[4,64,128]{2,1,0:T(8,128)S(1)}, f32[4,64,128]{2,1,0:T(8,128)S(1)}, u32[]{:S(2)}, u32[]{:S(2)}) collective-permute-start(f32[4,64,128]{2,1,0:T(8,128)S(1)} %get-tuple-element.107), channel_id=1, source_target_pairs={{8,16},{16,8},{24,32},{32,24},{40,48},{48,40},{56,64},{64,56},{72,... | collective-permute-start | bytes 393224 | tf_op jit(solution)/shard_map/cond/branch_3_fun/ppermute | solution.py:571
  89.7 0.0 collective-permute-done.2.first
  89.7 3.6 %collective-permute-done.3.second = f32[4,64,128]{2,1,0:T(8,128)S(1)} collective-permute-done((f32[4,64,128]{2,1,0:T(8,128)S(1)}, f32[4,64,128]{2,1,0:T(8,128)S(1)}, u32[]{:S(2)}, u32[]{:S(2)}) %collective-permute-start.3) | collective-permute-done | bytes 131104 | tf_op jit(solution)/shard_map/cond/branch_3_fun/ppermute | solution.py:571
  93.3 0.3 complete.8
  93.7 0.1 collective-permute-start.4
  93.8 4.6 %collective-permute-start.5 = (f32[4,2,64,128]{3,2,1,0:T(8,128)S(1)}, f32[4,2,64,128]{3,2,1,0:T(8,128)S(1)}, u32[]{:S(2)}, u32[]{:S(2)}) collective-permute-start(f32[4,2,64,128]{3,2,1,0:T(8,128)S(1)} %get-tuple-element.108.refs_3_), channel_id=1, source_target_pairs={{1,2},{2,1},{3,4},{4,3},{5,6},{6,5},{9,10},{10,9},{11,12},{12,11},... | collective-permute-start | bytes 786440 | tf_op jit(solution)/shard_map/cond/branch_3_fun/ppermute | solution.py:571
  98.4 0.0 collective-permute-done.4.refs_4_
  98.4 4.0 %collective-permute-done.5.refs_5_ = f32[4,2,64,128]{3,2,1,0:T(8,128)S(1)} collective-permute-done((f32[4,2,64,128]{3,2,1,0:T(8,128)S(1)}, f32[4,2,64,128]{3,2,1,0:T(8,128)S(1)}, u32[]{:S(2)}, u32[]{:S(2)}) %collective-permute-start.5) | collective-permute-done | bytes 262176 | tf_op jit(solution)/shard_map/cond/branch_3_fun/ppermute | solution.py:571
  102.4 0.0 collective-permute-done.refs_1_
  102.4 0.0 collective-permute-done.1.refs_2_
  102.4 9.3 %advect_both.8 = f32[4,10,64,128]{3,2,1,0:T(8,128)S(1)} custom-call(f32[4,8,64,128]{3,2,1,0:T(8,128)S(1)} %get-tuple-element.104.refs_0_, f32[4,8,64,128]{3,2,1,0:T(8,128)S(1)} %collective-permute-done.refs_1_, f32[4,8,64,128]{3,2,1,0:T(8,128)S(1)} %collective-permute-done.1.refs_2_, f32[4,2,64,128]{3,2,1,0:T(8,128)S(1)} %get-tuple-element.108.refs_3_, ...), custom_call_target="tpu_custom_call" | custom-call | tf_op jit(solution)/shard_map/cond/branch_3_fun/advect_both/pallas_call | solution.py:383
  111.9 12.4 %conditional.3 = (f32[8,64,4,128]{3,2,1,0:T(4,128)S(1)}) conditional(s32[]{:T(128)} %bitcast.4, (f32[4,10,64,128]{3,2,1,0:T(8,128)S(1)}, f32[12,10,64,128]{3,2,1,0:T(8,128)}) %tuple.40, (f32[4,10,64,128]{3,2,1,0:T(8,128)S(1)}, f32[12,10,64,128]{3,2,1,0:T(8,128)}) %tuple.40, (f32[4,10,64,128]{3,2,1,0:T(8,128)S(1)}, ...), branch_computations={%region_4.5_spmd, %region_5.6_spmd, %region_6.7_spmd, %region_7.8_... | conditional | bytes 27525236 | solution.py:590
  111.9 0.1 fusion.6
  112.0 0.1 collective-permute-start.26
  112.1 4.1 %collective-permute-start.27 = (f32[1,10,64,128]{3,2,1,0:T(8,128)S(1)}, f32[1,10,64,128]{3,2,1,0:T(8,128)S(1)}, u32[]{:S(2)}, u32[]{:S(2)}) collective-permute-start(f32[1,10,64,128]{3,2,1,0:T(8,128)S(1)} %get-tuple-element.185), channel_id=1, source_target_pairs={{1,2},{2,1},{3,4},{4,3},{5,6},{6,5},{9,10},{10,9},{11,12},{12,11},... | collective-permute-start | bytes 983048 | tf_op jit(solution)/shard_map/cond/branch_0_fun/ppermute | solution.py:571
  116.2 0.0 collective-permute-done.26.refs_1_
  116.2 4.7 %collective-permute-done.27.refs_2_ = f32[1,10,64,128]{3,2,1,0:T(8,128)S(1)} collective-permute-done((f32[1,10,64,128]{3,2,1,0:T(8,128)S(1)}, f32[1,10,64,128]{3,2,1,0:T(8,128)S(1)}, u32[]{:S(2)}, u32[]{:S(2)}) %collective-permute-start.27) | collective-permute-done | bytes 327712 | tf_op jit(solution)/shard_map/cond/branch_0_fun/ppermute | solution.py:571
  121.0 3.4 %advect_native.4 = f32[8,256,128]{2,1,0:T(8,128)S(1)} custom-call(f32[4,10,64,128]{3,2,1,0:T(8,128)S(1)} %get-tuple-element.112.refs_0_, f32[1,10,64,128]{3,2,1,0:T(8,128)S(1)} %collective-permute-done.26.refs_1_, f32[1,10,64,128]{3,2,1,0:T(8,128)S(1)} %collective-permute-done.27.refs_2_, f32[12,10,64,128]{3,2,1,0:T(8,128)} %get-tuple-element.113.refs_3_), custom_call_target="tpu_custom_call" | custom-call | tf_op jit(solution)/shard_map/cond/branch_0_fun/advect_native/pallas_call | solution.py:383
  124.3 0.0 copy-start.10
  124.4 1.0 copy-done.10
  (12 shorter events, 0.0 us)
Async XLA Ops:
  0.0 0.7 copy-start.7
  3.3 27.0 %collective-permute-start.32 = (f32[4,11,64,128]{3,2,1,0:T(8,128)S(1)}, f32[4,11,64,128]{3,2,1,0:T(8,128)}, u32[]{:S(2)}, u32[]{:S(2)}) collective-permute-start(f32[4,11,64,128]{3,2,1,0:T(8,128)S(1)} %get-tuple-element.146.own.refs_1_), channel_id=1, source_target_pairs={{0,1},{1,0},{2,3},{3,2},{4,5},{5,4},{6,7},{7,6},{8,9},{9,8},{10,11... | collective-permute-start | bytes 4325384 | tf_op jit(solution)/shard_map/ppermute | solution.py:571
  4.8 25.6 %collective-permute-start.33 = (f32[4,11,64,128]{3,2,1,0:T(8,128)S(1)}, f32[4,11,64,128]{3,2,1,0:T(8,128)}, u32[]{:S(2)}, u32[]{:S(2)}) collective-permute-start(f32[4,11,64,128]{3,2,1,0:T(8,128)S(1)} %get-tuple-element.146.own.refs_1_), channel_id=1, source_target_pairs={{1,2},{2,1},{3,4},{4,3},{5,6},{6,5},{9,10},{10,9},{11,12},{12,11},... | collective-permute-start | bytes 4325384 | tf_op jit(solution)/shard_map/ppermute | solution.py:571
  8.0 9.1 %collective-permute-start.34 = (f32[3,64,128]{2,1,0:T(8,128)S(1)}, f32[3,64,128]{2,1,0:T(8,128)S(1)}, u32[]{:S(2)}, u32[]{:S(2)}) collective-permute-start(f32[3,64,128]{2,1,0:T(8,128)S(1)} %get-tuple-element.148), channel_id=1, source_target_pairs={{0,8},{8,0},{16,24},{24,16},{32,40},{40,32},{48,56},{56,48},{64,72... | collective-permute-start | bytes 294920 | tf_op jit(solution)/shard_map/ppermute | solution.py:571
  9.7 7.4 %collective-permute-start.35 = (f32[3,64,128]{2,1,0:T(8,128)S(1)}, f32[3,64,128]{2,1,0:T(8,128)S(1)}, u32[]{:S(2)}, u32[]{:S(2)}) collective-permute-start(f32[3,64,128]{2,1,0:T(8,128)S(1)} %get-tuple-element.149), channel_id=1, source_target_pairs={{8,16},{16,8},{24,32},{32,24},{40,48},{48,40},{56,64},{64,56},{72,... | collective-permute-start | bytes 294920 | tf_op jit(solution)/shard_map/ppermute | solution.py:571
  17.4 12.4 %copy-start.12 = (s32[2]{0:T(128)S(1)}, s32[2]{0:T(128)}, u32[]{:S(2)}) copy-start(s32[2]{0:T(128)} %param.24) | copy-start | bytes 28
  17.4 12.9 %collective-permute-start.36 = (f32[4,3,64,128]{3,2,1,0:T(8,128)S(1)}, f32[4,3,64,128]{3,2,1,0:T(8,128)S(1)}, u32[]{:S(2)}, u32[]{:S(2)}) collective-permute-start(f32[4,3,64,128]{3,2,1,0:T(8,128)S(1)} %complete.9.sown.refs_4_), channel_id=1, source_target_pairs={{0,1},{1,0},{2,3},{3,2},{4,5},{5,4},{6,7},{7,6},{8,9},{9,8},{10,11... | collective-permute-start | bytes 1179656 | tf_op jit(solution)/shard_map/ppermute | solution.py:571
  17.5 12.8 %collective-permute-start.37 = (f32[4,3,64,128]{3,2,1,0:T(8,128)S(1)}, f32[4,3,64,128]{3,2,1,0:T(8,128)S(1)}, u32[]{:S(2)}, u32[]{:S(2)}) collective-permute-start(f32[4,3,64,128]{3,2,1,0:T(8,128)S(1)} %complete.9.sown.refs_4_), channel_id=1, source_target_pairs={{1,2},{2,1},{3,4},{4,3},{5,6},{6,5},{9,10},{10,9},{11,12},{12,11},... | collective-permute-start | bytes 1179656 | tf_op jit(solution)/shard_map/ppermute | solution.py:571
  21.7 32.4 %all-to-all-start = ((f32[128,24,128]{2,1,0:T(8,128)}), f32[128,24,128]{2,1,0:T(8,128)}, u32[]{:S(2)}, u32[]{:S(2)}) async-start(f32[128,24,128]{2,1,0:T(8,128)} %bitcast.11), calls=%async_computation | async-start | bytes 3145728 | tf_op jit(solution)/shard_map/all_to_all | solution.py:597
  30.3 6.0 %copy-start.2 = (f32[4,3,64,128]{3,2,1,0:T(8,128)}, f32[4,3,64,128]{3,2,1,0:T(8,128)S(1)}, u32[]{:S(2)}) copy-start(f32[4,3,64,128]{3,2,1,0:T(8,128)S(1)} %collective-permute-done.37.s1.refs_6_) | copy-start | bytes 1179652
  36.3 10.5 %copy-start = (f32[12,10,64,128]{3,2,1,0:T(8,128)}, f32[12,10,64,128]{3,2,1,0:T(8,128)S(1)}, u32[]{:S(2)}) copy-start(f32[12,10,64,128]{3,2,1,0:T(8,128)S(1)} %get-tuple-element.153.refs_7_.forward.refs_4_) | copy-start | bytes 11796484
  36.3 1.3 %copy-start.3 = (f32[4,3,64,128]{3,2,1,0:T(8,128)S(1)}, f32[4,3,64,128]{3,2,1,0:T(8,128)}, u32[]{:S(2)}) copy-start(f32[4,3,64,128]{3,2,1,0:T(8,128)} %copy-done.2) | copy-start | bytes 1179652
  37.6 7.9 %copy-start.11 = (f32[616]{0:T(1024)S(1)}, f32[616]{0:T(1024)}, u32[]{:S(2)}) copy-start(f32[616]{0:T(1024)} %param.28) | copy-start | bytes 7396
  41.7 20.0 %collective-permute-start.38 = (f32[4,10,64,128]{3,2,1,0:T(8,128)S(1)}, f32[4,10,64,128]{3,2,1,0:T(8,128)S(1)}, u32[]{:S(2)}, u32[]{:S(2)}) collective-permute-start(f32[4,10,64,128]{3,2,1,0:T(8,128)S(1)} %advect_both.9.field.refs_1_), channel_id=1, source_target_pairs={{0,1},{1,0},{2,3},{3,2},{4,5},{5,4},{6,7},{7,6},{8,9},{9,8},{10,11... | collective-permute-start | bytes 3932168 | tf_op jit(solution)/shard_map/ppermute | solution.py:571
  42.9 20.2 %collective-permute-start.39 = (f32[4,10,64,128]{3,2,1,0:T(8,128)S(1)}, f32[4,10,64,128]{3,2,1,0:T(8,128)}, u32[]{:S(2)}, u32[]{:S(2)}) collective-permute-start(f32[4,10,64,128]{3,2,1,0:T(8,128)S(1)} %advect_both.9.field.refs_1_), channel_id=1, source_target_pairs={{1,2},{2,1},{3,4},{4,3},{5,6},{6,5},{9,10},{10,9},{11,12},{12,11},... | collective-permute-start | bytes 3932168 | tf_op jit(solution)/shard_map/ppermute | solution.py:571
  46.8 7.3 %copy-start.4 = (s32[512]{0:T(512)S(1)}, s32[512]{0:T(512)}, u32[]{:S(2)}) copy-start(s32[512]{0:T(512)} %param.25) | copy-start | bytes 6148
  46.8 7.3 %copy-start.5 = (s32[2,128]{1,0:T(2,128)S(1)}, s32[2,128]{1,0:T(2,128)}, u32[]{:S(2)}) copy-start(s32[2,128]{1,0:T(2,128)} %cells.3) | copy-start | bytes 3076
  46.8 7.3 %copy-start.6 = (s32[2,128,1]{1,2,0:T(1,128)S(1)}, s32[2,128,1]{1,2,0:T(1,128)}, u32[]{:S(2)}) copy-start(s32[2,128,1]{1,2,0:T(1,128)} %param.23) | copy-start | bytes 3076
  54.1 9.0 %copy-start.1 = (f32[12,10,64,128]{3,2,1,0:T(8,128)S(1)}, f32[12,10,64,128]{3,2,1,0:T(8,128)}, u32[]{:S(2)}) copy-start(f32[12,10,64,128]{3,2,1,0:T(8,128)} %copy-done) | copy-start | bytes 11796484
  74.1 6.9 %copy-start.8 = (f32[12,10,64,128]{3,2,1,0:T(8,128)S(1)}, f32[12,10,64,128]{3,2,1,0:T(8,128)}, u32[]{:S(2)}) copy-start(f32[12,10,64,128]{3,2,1,0:T(8,128)} %adjoint_coefficients.1) | copy-start | bytes 11796484
  81.0 21.4 %collective-permute-start = (f32[4,8,64,128]{3,2,1,0:T(8,128)S(1)}, f32[4,8,64,128]{3,2,1,0:T(8,128)S(1)}, u32[]{:S(2)}, u32[]{:S(2)}) collective-permute-start(f32[4,8,64,128]{3,2,1,0:T(8,128)S(1)} %get-tuple-element.104.refs_0_), channel_id=1, source_target_pairs={{0,1},{1,0},{2,3},{3,2},{4,5},{5,4},{6,7},{7,6},{8,9},{9,8},{10,11... | collective-permute-start | bytes 3145736 | tf_op jit(solution)/shard_map/cond/branch_3_fun/ppermute | solution.py:571
  81.1 21.3 %collective-permute-start.1 = (f32[4,8,64,128]{3,2,1,0:T(8,128)S(1)}, f32[4,8,64,128]{3,2,1,0:T(8,128)S(1)}, u32[]{:S(2)}, u32[]{:S(2)}) collective-permute-start(f32[4,8,64,128]{3,2,1,0:T(8,128)S(1)} %get-tuple-element.104.refs_0_), channel_id=1, source_target_pairs={{1,2},{2,1},{3,4},{4,3},{5,6},{6,5},{9,10},{10,9},{11,12},{12,11},... | collective-permute-start | bytes 3145736 | tf_op jit(solution)/shard_map/cond/branch_3_fun/ppermute | solution.py:571
  85.1 4.7 %collective-permute-start.2 = (f32[4,64,128]{2,1,0:T(8,128)S(1)}, f32[4,64,128]{2,1,0:T(8,128)S(1)}, u32[]{:S(2)}, u32[]{:S(2)}) collective-permute-start(f32[4,64,128]{2,1,0:T(8,128)S(1)} %get-tuple-element.106), channel_id=1, source_target_pairs={{0,8},{8,0},{16,24},{24,16},{32,40},{40,32},{48,56},{56,48},{64,72... | collective-permute-start | bytes 393224 | tf_op jit(solution)/shard_map/cond/branch_3_fun/ppermute | solution.py:571
  86.2 7.1 %collective-permute-start.3 = (f32[4,64,128]{2,1,0:T(8,128)S(1)}, f32[4,64,128]{2,1,0:T(8,128)S(1)}, u32[]{:S(2)}, u32[]{:S(2)}) collective-permute-start(f32[4,64,128]{2,1,0:T(8,128)S(1)} %get-tuple-element.107), channel_id=1, source_target_pairs={{8,16},{16,8},{24,32},{32,24},{40,48},{48,40},{56,64},{64,56},{72,... | collective-permute-start | bytes 393224 | tf_op jit(solution)/shard_map/cond/branch_3_fun/ppermute | solution.py:571
  93.7 4.7 %collective-permute-start.4 = (f32[4,2,64,128]{3,2,1,0:T(8,128)S(1)}, f32[4,2,64,128]{3,2,1,0:T(8,128)S(1)}, u32[]{:S(2)}, u32[]{:S(2)}) collective-permute-start(f32[4,2,64,128]{3,2,1,0:T(8,128)S(1)} %get-tuple-element.108.refs_3_), channel_id=1, source_target_pairs={{0,1},{1,0},{2,3},{3,2},{4,5},{5,4},{6,7},{7,6},{8,9},{9,8},{10,11... | collective-permute-start | bytes 786440 | tf_op jit(solution)/shard_map/cond/branch_3_fun/ppermute | solution.py:571
  93.8 8.7 %collective-permute-start.5 = (f32[4,2,64,128]{3,2,1,0:T(8,128)S(1)}, f32[4,2,64,128]{3,2,1,0:T(8,128)S(1)}, u32[]{:S(2)}, u32[]{:S(2)}) collective-permute-start(f32[4,2,64,128]{3,2,1,0:T(8,128)S(1)} %get-tuple-element.108.refs_3_), channel_id=1, source_target_pairs={{1,2},{2,1},{3,4},{4,3},{5,6},{6,5},{9,10},{10,9},{11,12},{12,11},... | collective-permute-start | bytes 786440 | tf_op jit(solution)/shard_map/cond/branch_3_fun/ppermute | solution.py:571
  112.0 4.2 %collective-permute-start.26 = (f32[1,10,64,128]{3,2,1,0:T(8,128)S(1)}, f32[1,10,64,128]{3,2,1,0:T(8,128)S(1)}, u32[]{:S(2)}, u32[]{:S(2)}) collective-permute-start(f32[1,10,64,128]{3,2,1,0:T(8,128)S(1)} %get-tuple-element.186), channel_id=1, source_target_pairs={{0,1},{1,0},{2,3},{3,2},{4,5},{5,4},{6,7},{7,6},{8,9},{9,8},{10,11... | collective-permute-start | bytes 983048 | tf_op jit(solution)/shard_map/cond/branch_0_fun/ppermute | solution.py:571
  112.1 8.9 %collective-permute-start.27 = (f32[1,10,64,128]{3,2,1,0:T(8,128)S(1)}, f32[1,10,64,128]{3,2,1,0:T(8,128)S(1)}, u32[]{:S(2)}, u32[]{:S(2)}) collective-permute-start(f32[1,10,64,128]{3,2,1,0:T(8,128)S(1)} %get-tuple-element.185), channel_id=1, source_target_pairs={{1,2},{2,1},{3,4},{4,3},{5,6},{6,5},{9,10},{10,9},{11,12},{12,11},... | collective-permute-start | bytes 983048 | tf_op jit(solution)/shard_map/cond/branch_0_fun/ppermute | solution.py:571
  124.3 1.0 copy-start.10
where the time goes:
time: 126 us; the launch traced here: 125 us
  Pallas kernels  56.4 us (45%)
  starting transfers between devices  44.5 us (35%)
  waiting for transfers between devices  18.9 us (15%)
  local copies, waits for them, and re-layouts  3.62 us (3%)
  between operations  1.53 us (1%)
    ppermute x16, starting transfers between devices, swap(): return lax.ppermute(x, axis, pairs)  36.5 us
    pallas_call x4, Pallas kernels, advect(): pl.pallas_call(partial(advect_kernel, steps=steps if static else None, ap...  27.7 us
    pallas_call x2, Pallas kernels, observe(): pl.pallas_call(partial(observe_kernel, slot=slot), in_specs=[VMEM_SPEC] *...  14.4 us
    ppermute x16, waiting for transfers between devices, swap(): return lax.ppermute(x, axis, pairs)  13.8 us
    all_to_all x1, starting transfers between devices, per_device(): lax.all_to_all(sent, ('lon', 'lat'), split_axis=0, concat_axis=0, tiled=T...  7.98 us
    pallas_call x1, Pallas kernels, coefficients(): pl.pallas_call(coefficient_kernel, in_specs=[VMEM_SPEC] * 6, out_specs=[V...  5.94 us
    all_to_all x1, waiting for transfers between devices, per_device(): lax.all_to_all(sent, ('lon', 'lat'), split_axis=0, concat_axis=0, tiled=T...  5.09 us
    unnamed x24, local copies, waits for them, and re-layouts  2.97 us
  transfers between devices with their start and end apart: 17, of which 5 were waited for; matrix products, arithmetic and copies ran while one was open for 0% of the time, Pallas kernels for 19%

commit v1 on v0

--- a/solution.py
+++ b/solution.py
@@ -12,7 +12,7 @@
 I32 = jnp.int32
 VARS = 8
 SPAN = 32
-STRIP_SPAN = 16
+STRIP_SPAN = 32
 LEV = 64
 MAXSTEP = 4
 SND = 128
@@ -188,40 +188,38 @@
             if n == 0:
                 half_west = jnp.where(lane == 0, roll(spread[0], 121) * 0.5, half_west)
                 dd_west = jnp.where(lane == 0, roll(spread[2], 121), dd_west)
-            a, b = half + dd, half - dd
-            a_west, b_west = half_west + dd_west, half_west - dd_west
-            half = w1 * 0.5
-            for m, value in enumerate((a, b_west, half + dd, half - dd)):
-                raw[i, 4 * n + m] = value
-            out[i, 5 * n] = 1.0 - a + b_west
-            out[i, 5 * n + 1] = -b
-            out[i, 5 * n + 2] = a_west
-
-    each_row(0, 4, lambda j: fill(3 - j, r0.at[j], s0.at[j]))
-    each_row(0, 4, lambda j: fill(4 + j, own.at[j], sown.at[j]))
-    each_row(0, 4, lambda j: fill(8 + j, r1.at[3 - j], s1.at[3 - j]))
-
-    def interface(i):
-        for n in range(2):
-            c, d = raw[i, 4 * n + 2], raw[i, 4 * n + 3]
-            c_next, d_next = raw[i + 1, 4 * n + 2], raw[i + 1, 4 * n + 3]
-            raw[i, 4 * n + 2] = jnp.where(flipped, -d_next, c)
-            raw[i, 4 * n + 3] = jnp.where(flipped, -c_next, d)
-
-    each_row(0, 11, interface)
+            lat_half = w1 * 0.5
+            values = half + dd, half - dd, half_west + dd_west, half_west - dd_west, lat_half + dd, lat_half - dd
+            for m, value in enumerate(values):
+                raw[i, 6 * n + m] = value
+
+    for first, target, main, strip in ((0, 3, r0, s0), (4, 4, own, sown), (8, 11, r1, s1)):
+        way = 1 if first == 4 else -1
+
+        def two(j):
+            for q in (2 * j, 2 * j + 1):
+                row = 3 - q if first == 8 else q
+                fill(first + q if first == 8 else target + way * q, main.at[row], strip.at[row])
+
+        each_row(0, 2, two)
 
     def combine(i):
         scale = jnp.where(i >= 8, open_side, 1.0)
         for n in range(2):
-            u, w = raw[i, 4 * n + 2], raw[i, 4 * n + 3]
-            u_before, w_before = raw[i - 1, 4 * n + 2], raw[i - 1, 4 * n + 3]
-            out[i, 5 * n] = (out[i, 5 * n] - u + w_before) * scale
-            out[i, 5 * n + 1] = out[i, 5 * n + 1] * scale
-            out[i, 5 * n + 2] = out[i, 5 * n + 2] * scale
-            out[i, 5 * n + 3] = -w * scale
-            out[i, 5 * n + 4] = u_before * scale
+            a, b, a_west, b_west = (raw[i, 6 * n + m] for m in range(4))
+            u, w = interface(raw, flipped, i, n)
+            u_before, w_before = interface(raw, flipped, i - 1, n)
+            values = 1.0 - a + b_west - u + w_before, -b, a_west, -w, u_before
+            for m, value in enumerate(values):
+                out[i, 5 * n + m] = value * scale
 
     each_row(1, 11, combine)
+
+
+def interface(raw, flipped, i, n):
+    u = jnp.where(flipped, -raw[i + 1, 6 * n + 5], raw[i, 6 * n + 4])
+    w = jnp.where(flipped, -raw[i + 1, 6 * n + 4], raw[i, 6 * n + 5])
+    return u, w
 
 
 def coefficients(tile, strips):
@@ -229,23 +227,24 @@
         coefficient_kernel,
         in_specs=[VMEM_SPEC] * 6,
         out_specs=[VMEM_SPEC] * 2,
-        out_shape=[struct(12, 10, LEV, 128), struct(12, 8, LEV, 128)],
+        out_shape=[struct(12, 10, LEV, 128), struct(12, 12, LEV, 128)],
         compiler_params=params(4),
         name="coefficients",
     )(*tile, *strips)
 
 
 def adjoint_kernel(forward, raw, out):
+    flipped = lat_even()
     open_side = open_to_next_chip()
 
     def combine(i):
         scale = jnp.where(i >= 8, open_side, 1.0)
         for n in range(2):
             out[i, 5 * n] = forward[i, 5 * n]
-            out[i, 5 * n + 1] = raw[i, 4 * n] * scale
-            out[i, 5 * n + 2] = -raw[i, 4 * n + 1] * scale
-            out[i, 5 * n + 3] = raw[i, 4 * n + 2] * scale
-            out[i, 5 * n + 4] = -raw[i - 1, 4 * n + 3] * scale
+            out[i, 5 * n + 1] = raw[i, 6 * n] * scale
+            out[i, 5 * n + 2] = -raw[i, 6 * n + 3] * scale
+            out[i, 5 * n + 3] = interface(raw, flipped, i, n)[0] * scale
+            out[i, 5 * n + 4] = -interface(raw, flipped, i - 1, n)[1] * scale
 
     each_row(1, 11, combine)
 
@@ -341,14 +340,16 @@
                 store(v, stencil(5 if v >= VARS else 0, v, f, east, west))
 
     def step(reach):
-        def one(i, carry):
-            def store(v, value):
-                work[1 - reach % 2][i, v] = value
-
-            row(work[reach % 2], i, False, store)
+        def two(j, carry):
+            for i in (4 - reach + 2 * j, 5 - reach + 2 * j):
+
+                def store(v, value):
+                    work[1 - reach % 2][i, v] = value
+
+                row(work[reach % 2], i, False, store)
             return carry
 
-        lax.fori_loop(4 - reach, 8 + reach, one, 0)
+        lax.fori_loop(0, 2 + reach, two, 0)
 
     for reach in (3, 2, 1):
         when(steps > reach, partial(step, reach))

time: 126 us -> 113 us (0.90); the launches traced: 125 us -> 115 us
  Pallas kernels: 56.4 us -> 45.1 us
  waiting for transfers between devices: 18.9 us -> 21.1 us
  starting transfers between devices: 44.5 us -> 43 us
    pallas_call x4, Pallas kernels: 27.7 us -> 18.6 us  [advect(): pl.pallas_call(partial(advect_kernel, steps=steps if static else None, ap...]
    ppermute x16, waiting for transfers between devices: 13.8 us -> 16.5 us  [swap(): return lax.ppermute(x, axis, pairs)]
  transfers between devices with their start and end apart: 17 -> 17, of which waited for: 5 -> 5; matrix products, arithmetic and copies ran while one was open for 0% -> 1% of each run, Pallas kernels for 19% -> 20%
where the time goes in v1:
time: 113 us; the launch traced here: 115 us
  Pallas kernels  45.1 us (40%)
  starting transfers between devices  43 us (38%)
  waiting for transfers between devices  21.1 us (19%)
  local copies, waits for them, and re-layouts  3.77 us (3%)
  between operations  1.53 us (1%)
    ppermute x16, starting transfers between devices, swap(): return lax.ppermute(x, axis, pairs)  35.4 us
    pallas_call x4, Pallas kernels, advect(): pl.pallas_call(partial(advect_kernel, steps=steps if static else None, ap...  18.6 us
    ppermute x16, waiting for transfers between devices, swap(): return lax.ppermute(x, axis, pairs)  16.5 us
    pallas_call x2, Pallas kernels, observe(): pl.pallas_call(partial(observe_kernel, slot=slot), in_specs=[VMEM_SPEC] *...  13.6 us
    all_to_all x1, starting transfers between devices, per_device(): lax.all_to_all(sent, ('lon', 'lat'), split_axis=0, concat_axis=0, tiled=T...  7.64 us
    pallas_call x1, Pallas kernels, coefficients(): pl.pallas_call(coefficient_kernel, in_specs=[VMEM_SPEC] * 6, out_specs=[V...  4.99 us
    all_to_all x1, waiting for transfers between devices, per_device(): lax.all_to_all(sent, ('lon', 'lat'), split_axis=0, concat_axis=0, tiled=T...  4.63 us
    unnamed x24, local copies, waits for them, and re-layouts  2.97 us
  transfers between devices with their start and end apart: 17, of which 5 were waited for; matrix products, arithmetic and copies ran while one was open for 1% of the time, Pallas kernels for 20%

profile of v1, /device:TPU:1, one launch (start us, length us, event | category | flops | bytes accessed | tf_op | source)
XLA Modules:
  0.0 114.9 jit_solution(1540569234186046582)
XLA Ops:
  0.0 0.7 copy-done.7
  0.7 2.2 %pack.1 = (f32[4,11,64,128]{3,2,1,0:T(8,128)S(1)}, f32[4,3,64,128]{3,2,1,0:T(8,128)S(1)}, f32[3,64,128]{2,1,0:T(8,128)S(1)}, f32[3,64,128]{2,1,0:T(8,128)S(1)}) custom-call(f32[8,256,128]{2,1,0:T(8,128)} %bitcast.22, f32[2,256,128]{2,1,0:T(8,128)} %bitcast.27, f32[4,128]{1,0:T(4,128)S(1)} %copy-done.7), custom_call_target="tpu_custom_call" | custom-call | tf_op jit(solution)/shard_map/pack/pallas_call | solution.py:118
  2.9 4.6 %collective-permute-start.33 = (f32[4,11,64,128]{3,2,1,0:T(8,128)S(1)}, f32[4,11,64,128]{3,2,1,0:T(8,128)}, u32[]{:S(2)}, u32[]{:S(2)}) collective-permute-start(f32[4,11,64,128]{3,2,1,0:T(8,128)S(1)} %get-tuple-element.146.own.refs_1_), channel_id=1, source_target_pairs={{1,2},{2,1},{3,4},{4,3},{5,6},{6,5},{9,10},{10,9},{11,12},{12,11},... | collective-permute-start | bytes 4325384 | tf_op jit(solution)/shard_map/ppermute | solution.py:572
  7.5 0.1 collective-permute-start.32
  7.6 1.7 %collective-permute-start.34 = (f32[3,64,128]{2,1,0:T(8,128)S(1)}, f32[3,64,128]{2,1,0:T(8,128)S(1)}, u32[]{:S(2)}, u32[]{:S(2)}) collective-permute-start(f32[3,64,128]{2,1,0:T(8,128)S(1)} %get-tuple-element.148), channel_id=1, source_target_pairs={{0,8},{8,0},{16,24},{24,16},{32,40},{40,32},{48,56},{56,48},{64,72... | collective-permute-start | bytes 294920 | tf_op jit(solution)/shard_map/ppermute | solution.py:572
  9.3 4.4 %collective-permute-start.35 = (f32[3,64,128]{2,1,0:T(8,128)S(1)}, f32[3,64,128]{2,1,0:T(8,128)S(1)}, u32[]{:S(2)}, u32[]{:S(2)}) collective-permute-start(f32[3,64,128]{2,1,0:T(8,128)S(1)} %get-tuple-element.149), channel_id=1, source_target_pairs={{8,16},{16,8},{24,32},{32,24},{40,48},{48,40},{56,64},{64,56},{72,... | collective-permute-start | bytes 294920 | tf_op jit(solution)/shard_map/ppermute | solution.py:572
  13.8 2.9 %relayout.1 = f32[3072,128]{1,0:T(8,128)} custom-call(f32[2,1,3,128,512]{4,3,2,1,0:T(8,128)} %bitcast.19), custom_call_target="tpu_custom_call" | custom-call | tf_op jit(solution)/shard_map/relayout/pallas_call | solution.py:425
  16.7 0.0 collective-permute-done.34.first
  16.7 0.0 collective-permute-done.35.second
  16.7 0.3 complete.9.sown.refs_4_
  17.0 0.0 copy-start.12
  17.0 4.4 %collective-permute-start.37 = (f32[4,3,64,128]{3,2,1,0:T(8,128)S(1)}, f32[4,3,64,128]{3,2,1,0:T(8,128)S(1)}, u32[]{:S(2)}, u32[]{:S(2)}) collective-permute-start(f32[4,3,64,128]{3,2,1,0:T(8,128)S(1)} %complete.9.sown.refs_4_), channel_id=1, source_target_pairs={{1,2},{2,1},{3,4},{4,3},{5,6},{6,5},{9,10},{10,9},{11,12},{12,11},... | collective-permute-start | bytes 1179656 | tf_op jit(solution)/shard_map/ppermute | solution.py:572
  21.4 0.1 collective-permute-start.36
  21.5 7.6 %all-to-all-start = ((f32[128,24,128]{2,1,0:T(8,128)}), f32[128,24,128]{2,1,0:T(8,128)}, u32[]{:S(2)}, u32[]{:S(2)}) async-start(f32[128,24,128]{2,1,0:T(8,128)} %bitcast.11), calls=%async_computation | async-start | bytes 3145728 | tf_op jit(solution)/shard_map/all_to_all | solution.py:598
  29.1 0.0 copy-done.12
  29.1 0.6 fusion.9
  29.7 0.0 collective-permute-done.37.s1.refs_6_
  29.7 0.0 collective-permute-done.36.s0.refs_5_
  29.7 0.0 collective-permute-done.33.r1.refs_3_
  29.7 0.0 collective-permute-done.32.r0.refs_2_
  29.7 5.0 %coefficients.1 = (f32[12,10,64,128]{3,2,1,0:T(8,128)S(1)}, f32[12,12,64,128]{3,2,1,0:T(8,128)S(1)}) custom-call(f32[4,11,64,128]{3,2,1,0:T(8,128)S(1)} %get-tuple-element.146.own.refs_1_, f32[4,11,64,128]{3,2,1,0:T(8,128)} %collective-permute-done.32.r0.refs_2_, f32[4,11,64,128]{3,2,1,0:T(8,128)} %collective-permute-done.33.r1.refs_3_, ...), custom_call_target="tpu_custom_call" | custom-call | tf_op jit(solution)/shard_map/coefficients/pallas_call | solution.py:226
  34.7 0.0 copy-done.2
  34.7 0.0 copy-start.3
  34.8 1.3 %copy-done.3 = f32[4,3,64,128]{3,2,1,0:T(8,128)S(1)} copy-done((f32[4,3,64,128]{3,2,1,0:T(8,128)S(1)}, f32[4,3,64,128]{3,2,1,0:T(8,128)}, u32[]{:S(2)}) %copy-start.3) | copy-done | bytes 393240
  36.0 5.6 %advect_both.9.field.refs_1_ = f32[4,10,64,128]{3,2,1,0:T(8,128)S(1)} custom-call(s32[1]{0:T(128)} %get-tuple-element.192.refs_0_, f32[4,11,64,128]{3,2,1,0:T(8,128)S(1)} %get-tuple-element.146.own.refs_1_, f32[4,11,64,128]{3,2,1,0:T(8,128)} %collective-permute-done.32.r0.refs_2_, f32[4,11,64,128]{3,2,1,0:T(8,128)} %collective-permute-done.33.r1.refs_3_, ...), custom_call_target="tpu_custom_call" | custom-call | tf_op jit(solution)/shard_map/advect_both/pallas_call | solution.py:384
  41.6 3.5 %collective-permute-start.39 = (f32[4,10,64,128]{3,2,1,0:T(8,128)S(1)}, f32[4,10,64,128]{3,2,1,0:T(8,128)S(1)}, u32[]{:S(2)}, u32[]{:S(2)}) collective-permute-start(f32[4,10,64,128]{3,2,1,0:T(8,128)S(1)} %advect_both.9.field.refs_1_), channel_id=1, source_target_pairs={{1,2},{2,1},{3,4},{4,3},{5,6},{6,5},{9,10},{10,9},{11,12},{12,11},... | collective-permute-start | bytes 3932168 | tf_op jit(solution)/shard_map/ppermute | solution.py:572
  45.2 0.1 collective-permute-start.38
  46.6 0.0 copy-start.4
  46.6 0.0 copy-start.5
  46.6 0.0 copy-start.6
  46.6 2.3 %adjoint_coefficients.1 = f32[12,10,64,128]{3,2,1,0:T(8,128)} custom-call(f32[12,10,64,128]{3,2,1,0:T(8,128)S(1)} %get-tuple-element.153.refs_7_.forward.refs_4_, f32[12,12,64,128]{3,2,1,0:T(8,128)S(1)} %get-tuple-element.155.raw), custom_call_target="tpu_custom_call" | custom-call | tf_op jit(solution)/shard_map/adjoint_coefficients/pallas_call | solution.py:253
  48.9 4.6 %all-to-all-done = f32[128,24,128]{2,1,0:T(8,128)} async-done(((f32[128,24,128]{2,1,0:T(8,128)}), f32[128,24,128]{2,1,0:T(8,128)}, u32[]{:S(2)}, u32[]{:S(2)}) %all-to-all-start) | async-done | bytes 1572896 | tf_op jit(solution)/shard_map/all_to_all | solution.py:598
  53.5 0.0 copy-done.4
  53.5 7.1 %observe.2 = (f32[4,8,64,128]{3,2,1,0:T(8,128)S(1)}, f32[4,2,64,128]{3,2,1,0:T(8,128)S(1)}, f32[2,64,128]{2,1,0:T(8,128)S(1)}, f32[2,64,128]{2,1,0:T(8,128)S(1)}...) custom-call(s32[2,128]{1,0:T(2,128)S(1)} %copy-done.5, ...), custom_call_target="tpu_custom_call" | custom-call | tf_op jit(solution)/shard_map/observe/pallas_call | solution.py:554
  60.6 1.6 %collective-permute-done.39.refs_3_ = f32[4,10,64,128]{3,2,1,0:T(8,128)S(1)} collective-permute-done((f32[4,10,64,128]{3,2,1,0:T(8,128)S(1)}, f32[4,10,64,128]{3,2,1,0:T(8,128)S(1)}, u32[]{:S(2)}, u32[]{:S(2)}) %collective-permute-start.39) | collective-permute-done | bytes 1310752 | tf_op jit(solution)/shard_map/ppermute | solution.py:572
  62.2 0.0 collective-permute-done.38.refs_2_
  62.2 0.0 copy-done.1
  62.2 5.0 %advect_main.1.field = f32[4,8,64,128]{3,2,1,0:T(8,128)S(1)} custom-call(s32[1]{0:T(128)} %get-tuple-element.191.refs_0_, f32[4,10,64,128]{3,2,1,0:T(8,128)S(1)} %advect_both.9.field.refs_1_, f32[4,10,64,128]{3,2,1,0:T(8,128)} %collective-permute-done.38.refs_2_, f32[4,10,64,128]{3,2,1,0:T(8,128)S(1)} %collective-permute-done.39.refs_3_, ...), custom_call_target="tpu_custom_call" | custom-call | tf_op jit(solution)/shard_map/advect_main/pallas_call | solution.py:384
  67.2 6.4 %observe.3 = (f32[4,8,64,128]{3,2,1,0:T(8,128)S(1)}, f32[4,4,64,128]{3,2,1,0:T(8,128)S(1)}, f32[4,64,128]{2,1,0:T(8,128)S(1)}, f32[4,64,128]{2,1,0:T(8,128)S(1)}) custom-call(s32[2,128]{1,0:T(2,128)S(1)} %copy-done.5, s32[2,128]{1,0:T(2,128)S(1)} %bitcast.18, s32[1,512]{1,0:T(1,128)S(1)} %bitcast.16, f32[1,640]{1,0:T(1,128)S(1)} %broadcast_in_dim.7.weight, ...), custom_call_target="tpu_custom_call" | custom-call | tf_op jit(solution)/shard_map/observe/pallas_call | solution.py:554
  73.6 23.3 %conditional.2 = (f32[4,10,64,128]{3,2,1,0:T(8,128)S(1)}) conditional(s32[]{:T(128)} %bitcast.5, (f32[4,8,64,128]{3,2,1,0:T(8,128)S(1)}, f32[4,64,128]{2,1,0:T(8,128)S(1)}, f32[4,64,128]{2,1,0:T(8,128)S(1)}, f32[4,4,64,128]{3,2,1,0:T(8,128)S(1)}, f32[12,10,64,128]{3,2,1,0:T(8,128)S(1)}, ...), branch_computations={%region_0.1_spmd, %region_1.2_spmd, %region_2.3_spmd, %region_3.4_... | conditional | bytes 12845304 | solution.py:591
  73.7 0.1 fusion.2
  73.8 3.1 %collective-permute-start.15 = (f32[2,8,64,128]{3,2,1,0:T(8,128)S(1)}, f32[2,8,64,128]{3,2,1,0:T(8,128)S(1)}, u32[]{:S(2)}, u32[]{:S(2)}) collective-permute-start(f32[2,8,64,128]{3,2,1,0:T(8,128)S(1)} %get-tuple-element.177), channel_id=1, source_target_pairs={{1,2},{2,1},{3,4},{4,3},{5,6},{6,5},{9,10},{10,9},{11,12},{12,11},... | collective-permute-start | bytes 1572872 | tf_op jit(solution)/shard_map/cond/branch_1_fun/ppermute | solution.py:572
  76.9 0.1 collective-permute-start.14
  77.0 1.3 %collective-permute-start.16 = (f32[4,64,128]{2,1,0:T(8,128)S(1)}, f32[4,64,128]{2,1,0:T(8,128)S(1)}, u32[]{:S(2)}, u32[]{:S(2)}) collective-permute-start(f32[4,64,128]{2,1,0:T(8,128)S(1)} %get-tuple-element.90), channel_id=1, source_target_pairs={{0,8},{8,0},{16,24},{24,16},{32,40},{40,32},{48,56},{56,48},{64,72... | collective-permute-start | bytes 393224 | tf_op jit(solution)/shard_map/cond/branch_1_fun/ppermute | solution.py:572
  78.3 3.4 %collective-permute-start.17 = (f32[4,64,128]{2,1,0:T(8,128)S(1)}, f32[4,64,128]{2,1,0:T(8,128)S(1)}, u32[]{:S(2)}, u32[]{:S(2)}) collective-permute-start(f32[4,64,128]{2,1,0:T(8,128)S(1)} %get-tuple-element.91), channel_id=1, source_target_pairs={{8,16},{16,8},{24,32},{32,24},{40,48},{48,40},{56,64},{64,56},{72,... | collective-permute-start | bytes 393224 | tf_op jit(solution)/shard_map/cond/branch_1_fun/ppermute | solution.py:572
  81.8 0.0 collective-permute-done.16.first
  81.8 4.2 %collective-permute-done.17.second = f32[4,64,128]{2,1,0:T(8,128)S(1)} collective-permute-done((f32[4,64,128]{2,1,0:T(8,128)S(1)}, f32[4,64,128]{2,1,0:T(8,128)S(1)}, u32[]{:S(2)}, u32[]{:S(2)}) %collective-permute-start.17) | collective-permute-done | bytes 131104 | tf_op jit(solution)/shard_map/cond/branch_1_fun/ppermute | solution.py:572
  86.0 0.3 complete.6
  86.4 4.7 %collective-permute-start.19 = (f32[2,2,64,128]{3,2,1,0:T(8,128)S(1)}, f32[2,2,64,128]{3,2,1,0:T(8,128)S(1)}, u32[]{:S(2)}, u32[]{:S(2)}) collective-permute-start(f32[2,2,64,128]{3,2,1,0:T(8,128)S(1)} %get-tuple-element.179), channel_id=1, source_target_pairs={{1,2},{2,1},{3,4},{4,3},{5,6},{6,5},{9,10},{10,9},{11,12},{12,11},... | collective-permute-start | bytes 393224 | tf_op jit(solution)/shard_map/cond/branch_1_fun/ppermute | solution.py:572
  91.0 0.1 collective-permute-start.18
  91.1 2.5 %collective-permute-done.19.refs_5_ = f32[2,2,64,128]{3,2,1,0:T(8,128)S(1)} collective-permute-done((f32[2,2,64,128]{3,2,1,0:T(8,128)S(1)}, f32[2,2,64,128]{3,2,1,0:T(8,128)S(1)}, u32[]{:S(2)}, u32[]{:S(2)}) %collective-permute-start.19) | collective-permute-done | bytes 131104 | tf_op jit(solution)/shard_map/cond/branch_1_fun/ppermute | solution.py:572
  93.7 0.0 collective-permute-done.18.refs_4_
  93.7 0.0 collective-permute-done.15.refs_2_
  93.7 0.0 collective-permute-done.14.refs_1_
  93.7 3.1 %advect_both.6 = f32[4,10,64,128]{3,2,1,0:T(8,128)S(1)} custom-call(f32[4,8,64,128]{3,2,1,0:T(8,128)S(1)} %get-tuple-element.88.refs_0_, f32[2,8,64,128]{3,2,1,0:T(8,128)S(1)} %collective-permute-done.14.refs_1_, f32[2,8,64,128]{3,2,1,0:T(8,128)S(1)} %collective-permute-done.15.refs_2_, f32[4,2,64,128]{3,2,1,0:T(8,128)S(1)} %get-tuple-element.92.refs_3_, ...), custom_call_target="tpu_custom_call" | custom-call | tf_op jit(solution)/shard_map/cond/branch_1_fun/advect_both/pallas_call | solution.py:384
  97.0 17.0 %conditional.3 = (f32[8,64,4,128]{3,2,1,0:T(4,128)S(1)}) conditional(s32[]{:T(128)} %bitcast.4, (f32[4,10,64,128]{3,2,1,0:T(8,128)S(1)}, f32[12,10,64,128]{3,2,1,0:T(8,128)}) %tuple.40, (f32[4,10,64,128]{3,2,1,0:T(8,128)S(1)}, f32[12,10,64,128]{3,2,1,0:T(8,128)}) %tuple.40, (f32[4,10,64,128]{3,2,1,0:T(8,128)S(1)}, ...), branch_computations={%region_4.5_spmd, %region_5.6_spmd, %region_6.7_spmd, %region_7.8_... | conditional | bytes 27525236 | solution.py:591
  97.0 0.1 fusion.7
  97.1 3.6 %collective-permute-start.29 = (f32[2,10,64,128]{3,2,1,0:T(8,128)S(1)}, f32[2,10,64,128]{3,2,1,0:T(8,128)S(1)}, u32[]{:S(2)}, u32[]{:S(2)}) collective-permute-start(f32[2,10,64,128]{3,2,1,0:T(8,128)S(1)} %get-tuple-element.187), channel_id=1, source_target_pairs={{1,2},{2,1},{3,4},{4,3},{5,6},{6,5},{9,10},{10,9},{11,12},{12,11},... | collective-permute-start | bytes 1966088 | tf_op jit(solution)/shard_map/cond/branch_1_fun/ppermute | solution.py:572
  100.7 0.1 collective-permute-start.28
  100.8 8.2 %collective-permute-done.29.refs_2_ = f32[2,10,64,128]{3,2,1,0:T(8,128)S(1)} collective-permute-done((f32[2,10,64,128]{3,2,1,0:T(8,128)S(1)}, f32[2,10,64,128]{3,2,1,0:T(8,128)S(1)}, u32[]{:S(2)}, u32[]{:S(2)}) %collective-permute-start.29) | collective-permute-done | bytes 655392 | tf_op jit(solution)/shard_map/cond/branch_1_fun/ppermute | solution.py:572
  109.0 0.0 collective-permute-done.28.refs_1_
  109.0 5.0 %advect_native.5 = f32[8,256,128]{2,1,0:T(8,128)S(1)} custom-call(f32[4,10,64,128]{3,2,1,0:T(8,128)S(1)} %get-tuple-element.114.refs_0_, f32[2,10,64,128]{3,2,1,0:T(8,128)S(1)} %collective-permute-done.28.refs_1_, f32[2,10,64,128]{3,2,1,0:T(8,128)S(1)} %collective-permute-done.29.refs_2_, f32[12,10,64,128]{3,2,1,0:T(8,128)} %get-tuple-element.115.refs_3_), custom_call_target="tpu_custom_call" | custom-call | tf_op jit(solution)/shard_map/cond/branch_1_fun/advect_native/pallas_call | solution.py:384
  114.0 0.0 copy-start.10
  114.0 1.0 copy-done.10
  (14 shorter events, 0.0 us)
Async XLA Ops:
  0.0 0.7 copy-start.7
  2.9 26.8 %collective-permute-start.33 = (f32[4,11,64,128]{3,2,1,0:T(8,128)S(1)}, f32[4,11,64,128]{3,2,1,0:T(8,128)}, u32[]{:S(2)}, u32[]{:S(2)}) collective-permute-start(f32[4,11,64,128]{3,2,1,0:T(8,128)S(1)} %get-tuple-element.146.own.refs_1_), channel_id=1, source_target_pairs={{1,2},{2,1},{3,4},{4,3},{5,6},{6,5},{9,10},{10,9},{11,12},{12,11},... | collective-permute-start | bytes 4325384 | tf_op jit(solution)/shard_map/ppermute | solution.py:572
  7.5 22.2 %collective-permute-start.32 = (f32[4,11,64,128]{3,2,1,0:T(8,128)S(1)}, f32[4,11,64,128]{3,2,1,0:T(8,128)}, u32[]{:S(2)}, u32[]{:S(2)}) collective-permute-start(f32[4,11,64,128]{3,2,1,0:T(8,128)S(1)} %get-tuple-element.146.own.refs_1_), channel_id=1, source_target_pairs={{0,1},{1,0},{2,3},{3,2},{4,5},{5,4},{6,7},{7,6},{8,9},{9,8},{10,11... | collective-permute-start | bytes 4325384 | tf_op jit(solution)/shard_map/ppermute | solution.py:572
  7.6 9.1 %collective-permute-start.34 = (f32[3,64,128]{2,1,0:T(8,128)S(1)}, f32[3,64,128]{2,1,0:T(8,128)S(1)}, u32[]{:S(2)}, u32[]{:S(2)}) collective-permute-start(f32[3,64,128]{2,1,0:T(8,128)S(1)} %get-tuple-element.148), channel_id=1, source_target_pairs={{0,8},{8,0},{16,24},{24,16},{32,40},{40,32},{48,56},{56,48},{64,72... | collective-permute-start | bytes 294920 | tf_op jit(solution)/shard_map/ppermute | solution.py:572
  9.3 7.4 %collective-permute-start.35 = (f32[3,64,128]{2,1,0:T(8,128)S(1)}, f32[3,64,128]{2,1,0:T(8,128)S(1)}, u32[]{:S(2)}, u32[]{:S(2)}) collective-permute-start(f32[3,64,128]{2,1,0:T(8,128)S(1)} %get-tuple-element.149), channel_id=1, source_target_pairs={{8,16},{16,8},{24,32},{32,24},{40,48},{48,40},{56,64},{64,56},{72,... | collective-permute-start | bytes 294920 | tf_op jit(solution)/shard_map/ppermute | solution.py:572
  17.0 12.1 %copy-start.12 = (s32[2]{0:T(128)S(1)}, s32[2]{0:T(128)}, u32[]{:S(2)}) copy-start(s32[2]{0:T(128)} %param.24) | copy-start | bytes 28
  17.0 12.7 %collective-permute-start.37 = (f32[4,3,64,128]{3,2,1,0:T(8,128)S(1)}, f32[4,3,64,128]{3,2,1,0:T(8,128)S(1)}, u32[]{:S(2)}, u32[]{:S(2)}) collective-permute-start(f32[4,3,64,128]{3,2,1,0:T(8,128)S(1)} %complete.9.sown.refs_4_), channel_id=1, source_target_pairs={{1,2},{2,1},{3,4},{4,3},{5,6},{6,5},{9,10},{10,9},{11,12},{12,11},... | collective-permute-start | bytes 1179656 | tf_op jit(solution)/shard_map/ppermute | solution.py:572
  21.4 8.3 %collective-permute-start.36 = (f32[4,3,64,128]{3,2,1,0:T(8,128)S(1)}, f32[4,3,64,128]{3,2,1,0:T(8,128)S(1)}, u32[]{:S(2)}, u32[]{:S(2)}) collective-permute-start(f32[4,3,64,128]{3,2,1,0:T(8,128)S(1)} %complete.9.sown.refs_4_), channel_id=1, source_target_pairs={{0,1},{1,0},{2,3},{3,2},{4,5},{5,4},{6,7},{7,6},{8,9},{9,8},{10,11... | collective-permute-start | bytes 1179656 | tf_op jit(solution)/shard_map/ppermute | solution.py:572
  21.5 32.0 %all-to-all-start = ((f32[128,24,128]{2,1,0:T(8,128)}), f32[128,24,128]{2,1,0:T(8,128)}, u32[]{:S(2)}, u32[]{:S(2)}) async-start(f32[128,24,128]{2,1,0:T(8,128)} %bitcast.11), calls=%async_computation | async-start | bytes 3145728 | tf_op jit(solution)/shard_map/all_to_all | solution.py:598
  29.7 5.0 %copy-start.2 = (f32[4,3,64,128]{3,2,1,0:T(8,128)}, f32[4,3,64,128]{3,2,1,0:T(8,128)S(1)}, u32[]{:S(2)}) copy-start(f32[4,3,64,128]{3,2,1,0:T(8,128)S(1)} %collective-permute-done.36.s0.refs_5_) | copy-start | bytes 1179652
  34.7 11.8 %copy-start = (f32[12,10,64,128]{3,2,1,0:T(8,128)}, f32[12,10,64,128]{3,2,1,0:T(8,128)S(1)}, u32[]{:S(2)}) copy-start(f32[12,10,64,128]{3,2,1,0:T(8,128)S(1)} %get-tuple-element.153.refs_7_.forward.refs_4_) | copy-start | bytes 11796484
  34.7 1.3 %copy-start.3 = (f32[4,3,64,128]{3,2,1,0:T(8,128)S(1)}, f32[4,3,64,128]{3,2,1,0:T(8,128)}, u32[]{:S(2)}) copy-start(f32[4,3,64,128]{3,2,1,0:T(8,128)} %copy-done.2) | copy-start | bytes 1179652
  36.0 10.5 %copy-start.11 = (f32[616]{0:T(1024)S(1)}, f32[616]{0:T(1024)}, u32[]{:S(2)}) copy-start(f32[616]{0:T(1024)} %param.28) | copy-start | bytes 7396
  41.6 20.6 %collective-permute-start.39 = (f32[4,10,64,128]{3,2,1,0:T(8,128)S(1)}, f32[4,10,64,128]{3,2,1,0:T(8,128)S(1)}, u32[]{:S(2)}, u32[]{:S(2)}) collective-permute-start(f32[4,10,64,128]{3,2,1,0:T(8,128)S(1)} %advect_both.9.field.refs_1_), channel_id=1, source_target_pairs={{1,2},{2,1},{3,4},{4,3},{5,6},{6,5},{9,10},{10,9},{11,12},{12,11},... | collective-permute-start | bytes 3932168 | tf_op jit(solution)/shard_map/ppermute | solution.py:572
  45.2 17.0 %collective-permute-start.38 = (f32[4,10,64,128]{3,2,1,0:T(8,128)S(1)}, f32[4,10,64,128]{3,2,1,0:T(8,128)}, u32[]{:S(2)}, u32[]{:S(2)}) collective-permute-start(f32[4,10,64,128]{3,2,1,0:T(8,128)S(1)} %advect_both.9.field.refs_1_), channel_id=1, source_target_pairs={{0,1},{1,0},{2,3},{3,2},{4,5},{5,4},{6,7},{7,6},{8,9},{9,8},{10,11... | collective-permute-start | bytes 3932168 | tf_op jit(solution)/shard_map/ppermute | solution.py:572
  46.6 6.9 %copy-start.4 = (s32[512]{0:T(512)S(1)}, s32[512]{0:T(512)}, u32[]{:S(2)}) copy-start(s32[512]{0:T(512)} %param.25) | copy-start | bytes 6148
  46.6 6.9 %copy-start.5 = (s32[2,128]{1,0:T(2,128)S(1)}, s32[2,128]{1,0:T(2,128)}, u32[]{:S(2)}) copy-start(s32[2,128]{1,0:T(2,128)} %cells.3) | copy-start | bytes 3076
  46.6 6.9 %copy-start.6 = (s32[2,128,1]{1,2,0:T(1,128)S(1)}, s32[2,128,1]{1,2,0:T(1,128)}, u32[]{:S(2)}) copy-start(s32[2,128,1]{1,2,0:T(1,128)} %param.23) | copy-start | bytes 3076
  53.5 8.7 %copy-start.1 = (f32[12,10,64,128]{3,2,1,0:T(8,128)S(1)}, f32[12,10,64,128]{3,2,1,0:T(8,128)}, u32[]{:S(2)}) copy-start(f32[12,10,64,128]{3,2,1,0:T(8,128)} %copy-done) | copy-start | bytes 11796484
  67.2 6.5 %copy-start.8 = (f32[12,10,64,128]{3,2,1,0:T(8,128)S(1)}, f32[12,10,64,128]{3,2,1,0:T(8,128)}, u32[]{:S(2)}) copy-start(f32[12,10,64,128]{3,2,1,0:T(8,128)} %adjoint_coefficients.1) | copy-start | bytes 11796484
  73.8 19.9 %collective-permute-start.15 = (f32[2,8,64,128]{3,2,1,0:T(8,128)S(1)}, f32[2,8,64,128]{3,2,1,0:T(8,128)S(1)}, u32[]{:S(2)}, u32[]{:S(2)}) collective-permute-start(f32[2,8,64,128]{3,2,1,0:T(8,128)S(1)} %get-tuple-element.177), channel_id=1, source_target_pairs={{1,2},{2,1},{3,4},{4,3},{5,6},{6,5},{9,10},{10,9},{11,12},{12,11},... | collective-permute-start | bytes 1572872 | tf_op jit(solution)/shard_map/cond/branch_1_fun/ppermute | solution.py:572
  76.9 16.8 %collective-permute-start.14 = (f32[2,8,64,128]{3,2,1,0:T(8,128)S(1)}, f32[2,8,64,128]{3,2,1,0:T(8,128)S(1)}, u32[]{:S(2)}, u32[]{:S(2)}) collective-permute-start(f32[2,8,64,128]{3,2,1,0:T(8,128)S(1)} %get-tuple-element.178), channel_id=1, source_target_pairs={{0,1},{1,0},{2,3},{3,2},{4,5},{5,4},{6,7},{7,6},{8,9},{9,8},{10,11... | collective-permute-start | bytes 1572872 | tf_op jit(solution)/shard_map/cond/branch_1_fun/ppermute | solution.py:572
  77.0 4.8 %collective-permute-start.16 = (f32[4,64,128]{2,1,0:T(8,128)S(1)}, f32[4,64,128]{2,1,0:T(8,128)S(1)}, u32[]{:S(2)}, u32[]{:S(2)}) collective-permute-start(f32[4,64,128]{2,1,0:T(8,128)S(1)} %get-tuple-element.90), channel_id=1, source_target_pairs={{0,8},{8,0},{16,24},{24,16},{32,40},{40,32},{48,56},{56,48},{64,72... | collective-permute-start | bytes 393224 | tf_op jit(solution)/shard_map/cond/branch_1_fun/ppermute | solution.py:572
  78.3 7.7 %collective-permute-start.17 = (f32[4,64,128]{2,1,0:T(8,128)S(1)}, f32[4,64,128]{2,1,0:T(8,128)S(1)}, u32[]{:S(2)}, u32[]{:S(2)}) collective-permute-start(f32[4,64,128]{2,1,0:T(8,128)S(1)} %get-tuple-element.91), channel_id=1, source_target_pairs={{8,16},{16,8},{24,32},{32,24},{40,48},{48,40},{56,64},{64,56},{72,... | collective-permute-start | bytes 393224 | tf_op jit(solution)/shard_map/cond/branch_1_fun/ppermute | solution.py:572
  86.4 7.3 %collective-permute-start.19 = (f32[2,2,64,128]{3,2,1,0:T(8,128)S(1)}, f32[2,2,64,128]{3,2,1,0:T(8,128)S(1)}, u32[]{:S(2)}, u32[]{:S(2)}) collective-permute-start(f32[2,2,64,128]{3,2,1,0:T(8,128)S(1)} %get-tuple-element.179), channel_id=1, source_target_pairs={{1,2},{2,1},{3,4},{4,3},{5,6},{6,5},{9,10},{10,9},{11,12},{12,11},... | collective-permute-start | bytes 393224 | tf_op jit(solution)/shard_map/cond/branch_1_fun/ppermute | solution.py:572
  91.0 2.6 %collective-permute-start.18 = (f32[2,2,64,128]{3,2,1,0:T(8,128)S(1)}, f32[2,2,64,128]{3,2,1,0:T(8,128)S(1)}, u32[]{:S(2)}, u32[]{:S(2)}) collective-permute-start(f32[2,2,64,128]{3,2,1,0:T(8,128)S(1)} %get-tuple-element.180), channel_id=1, source_target_pairs={{0,1},{1,0},{2,3},{3,2},{4,5},{5,4},{6,7},{7,6},{8,9},{9,8},{10,11... | collective-permute-start | bytes 393224 | tf_op jit(solution)/shard_map/cond/branch_1_fun/ppermute | solution.py:572
  97.1 11.9 %collective-permute-start.29 = (f32[2,10,64,128]{3,2,1,0:T(8,128)S(1)}, f32[2,10,64,128]{3,2,1,0:T(8,128)S(1)}, u32[]{:S(2)}, u32[]{:S(2)}) collective-permute-start(f32[2,10,64,128]{3,2,1,0:T(8,128)S(1)} %get-tuple-element.187), channel_id=1, source_target_pairs={{1,2},{2,1},{3,4},{4,3},{5,6},{6,5},{9,10},{10,9},{11,12},{12,11},... | collective-permute-start | bytes 1966088 | tf_op jit(solution)/shard_map/cond/branch_1_fun/ppermute | solution.py:572
  100.7 8.3 %collective-permute-start.28 = (f32[2,10,64,128]{3,2,1,0:T(8,128)S(1)}, f32[2,10,64,128]{3,2,1,0:T(8,128)S(1)}, u32[]{:S(2)}, u32[]{:S(2)}) collective-permute-start(f32[2,10,64,128]{3,2,1,0:T(8,128)S(1)} %get-tuple-element.188), channel_id=1, source_target_pairs={{0,1},{1,0},{2,3},{3,2},{4,5},{5,4},{6,7},{7,6},{8,9},{9,8},{10,11... | collective-permute-start | bytes 1966088 | tf_op jit(solution)/shard_map/cond/branch_1_fun/ppermute | solution.py:572
  114.0 1.0 copy-start.10
